TPU v7x, 512 devices: a whole 4x8x8 slice. The times are simulated.
512 devices in a mesh: grp: 16 (over z_hi, y), seq: 32 (over x, z_lo, core).
Axes of the slice: x: 4, y: 8, z: 8 (z_hi: 2, z_lo: 4; z = z_hi * 4 + z_lo), core: 2. Of those that a mesh axis runs over, the one named last changes fastest.
Arguments:
- tokens: bfloat16 [65536, 2048], P(('grp', 'seq')), may hold values from -6.6 to 6.6
- grad_output: bfloat16 [65536, 2048], P(('grp', 'seq')), may hold values from -6 to 6
- query_gain: float32 [2048], replicated, may hold values from -6 to 6
- key_gain: float32 [2048], replicated, may hold values from -6 to 6
- short_query_gain: float32 [2048], replicated, may hold values from -24 to 24
- short_key_gain: float32 [2048], replicated, may hold values from -24 to 24
Outputs:
- grad_tokens: bfloat16 [65536, 2048], P(('grp', 'seq'))
- gain_grads: float32 [4, 2048], replicated
All inputs are finite; a program needn't handle non-finite values.
Results may differ from a plain program's by a relative error of at most 0.019.
Values may be sent and summed in bfloat16 or wider, within the bound.
A program may use at most 64 MiB of HBM per device.

v0:
```python
import jax
import jax.numpy as jnp
from jax import lax
from jax.sharding import Mesh
from jax.sharding import PartitionSpec as P

HEADS = 16
WINDOW = 128
SHORTEN = 16
GRP_SEQ = ("grp_0", "grp_1", "seq_0", "seq_1", "seq_2")
GRP = ("grp_0", "grp_1")
SEQ = ("seq_0", "seq_1", "seq_2")


NEGATIVE = -1e30


def shifted_2(value, axis, steps):
    count = lax.axis_size(axis)
    leading, last = (max(0, -steps), min(count, count - steps))
    return lax.ppermute(value, axis, [(source, source + steps) for source in range(leading, last)])


def side_by_side(arrays, axis, split_dim, concat_dim, along):
    widths = [a.shape[along] for a in arrays]
    both = jnp.concatenate(arrays, axis=along)
    filled = lax.all_to_all(both, axis, split_axis=split_dim, concat_axis=concat_dim, tiled=True)
    return tuple(jnp.split(filled, [sum(widths[:k]) for k in range(1, len(widths))], axis=along))


def in_one_piece(arrays, axis, dim, along):
    ends, at = ([], 0)
    for a in arrays[:-1]:
        at += a.shape[along]
        ends.append(at)
    both = jnp.concatenate(arrays, axis=along)
    return tuple(jnp.split(lax.all_gather(both, axis, axis=dim, tiled=True), ends, axis=along))


def one_axis_at_a_time(x, axes):
    for axis in axes:
        x = lax.psum(x, axis)
    return x


def head_scores(queries, key_rows):
    temper = queries.shape[-1] ** (-0.5)
    return (
        jnp.einsum("qhe,khe->hqk", queries, key_rows, preferred_element_type=jnp.float32) * temper
    )


def short_order(absolute, block_rows, group_rows, seq_count):
    within = absolute % group_rows
    source = absolute // group_rows
    return (within // block_rows * seq_count + source) * block_rows + within % block_rows


def shards(tokens, grad_output, query_gain, key_gain, short_query_gain, short_key_gain):
    local_rows, model_width = tokens.shape
    head_size = model_width // HEADS
    temper = head_size ** (-0.5)
    chain_index = lax.axis_index(GRP_SEQ)
    token_f = tokens.astype(jnp.float32)
    query_heads = (token_f * query_gain).astype(jnp.bfloat16).reshape(local_rows, HEADS, head_size)
    prior_rows = shifted_2(tokens, GRP_SEQ, 1)
    context = jnp.concatenate([prior_rows, tokens], axis=0)
    context_f = context.astype(jnp.float32)
    key_heads = (
        (context_f * key_gain).astype(jnp.bfloat16).reshape(local_rows + WINDOW, HEADS, head_size)
    )
    value_heads = context.reshape(local_rows + WINDOW, HEADS, head_size)
    query_pos = chain_index * local_rows + jnp.arange(local_rows, dtype=jnp.int32)[:, None]
    key_pos = (
        chain_index * local_rows
        - WINDOW
        + jnp.arange(local_rows + WINDOW, dtype=jnp.int32)[None, :]
    )
    allowed = (key_pos <= query_pos) & (key_pos > query_pos - WINDOW) & (key_pos >= 0)
    scores = jnp.where(allowed[None], head_scores(query_heads, key_heads), NEGATIVE)
    log_total = jax.nn.logsumexp(scores, axis=-1)
    weights = jnp.where(allowed[None], jnp.exp(scores - log_total[..., None]), 0.0)
    weights_low = weights.astype(jnp.bfloat16)
    local_out = jnp.einsum(
        "hqk,khe->qhe", weights_low, value_heads, preferred_element_type=jnp.float32
    ).reshape(local_rows, model_width)
    mixed_rows = (token_f + local_out).astype(jnp.bfloat16)
    tail_rows = shifted_2(mixed_rows[local_rows - (SHORTEN - 1) :], GRP_SEQ, 1)
    shifted = jnp.concatenate([tail_rows, mixed_rows], axis=0)[:local_rows]
    short_rows = local_rows // SHORTEN
    pooled = (
        shifted.astype(jnp.float32).reshape(short_rows, SHORTEN, model_width).sum(axis=1)
        * (1.0 / SHORTEN)
    ).astype(jnp.bfloat16)
    grad_short = (
        grad_output.astype(jnp.float32)
        .reshape(short_rows, SHORTEN, model_width)
        .sum(axis=1)
        .astype(jnp.bfloat16)
    )
    groups = lax.axis_size(GRP)
    seq_count = lax.axis_size(SEQ)
    group_index = lax.axis_index(GRP)
    seq_index = lax.axis_index(SEQ)
    head_width = model_width // groups
    head_part = head_width // head_size
    group_rows = short_rows * groups
    pooled_here, grad_here = side_by_side(
        (
            pooled.reshape(short_rows, groups, head_width),
            grad_short.reshape(short_rows, groups, head_width),
        ),
        GRP,
        1,
        0,
        2,
    )
    pooled_here = pooled_here.reshape(group_rows, head_width)
    grad_here = grad_here.reshape(group_rows, head_width)
    gain_query = lax.dynamic_slice_in_dim(short_query_gain, group_index * head_width, head_width)
    gain_key = lax.dynamic_slice_in_dim(short_key_gain, group_index * head_width, head_width)
    pooled_f = pooled_here.astype(jnp.float32)
    short_queries = (
        (pooled_f * gain_query).astype(jnp.bfloat16).reshape(group_rows, head_part, head_size)
    )
    short_keys = (
        (pooled_f * gain_key).astype(jnp.bfloat16).reshape(group_rows, head_part, head_size)
    )
    short_values = pooled_here.reshape(group_rows, head_part, head_size)
    short_incoming = grad_here.reshape(group_rows, head_part, head_size)
    own_pos = short_order(
        seq_index * group_rows + jnp.arange(group_rows, dtype=jnp.int32),
        short_rows,
        group_rows,
        seq_count,
    )
    peak = jnp.full((head_part, group_rows), NEGATIVE, jnp.float32)
    fetched_keys, fetched_values = in_one_piece((short_keys, short_values), SEQ, 0, 1)
    remote_pos = short_order(
        jnp.arange(fetched_keys.shape[0], dtype=jnp.int32), short_rows, group_rows, seq_count
    )
    visible = remote_pos[None, :] <= own_pos[:, None]
    piece_scores = jnp.where(visible[None], head_scores(short_queries, fetched_keys), NEGATIVE)
    highest = jnp.maximum(peak, piece_scores.max(axis=-1))
    piece_weights = jnp.where(visible[None], jnp.exp(piece_scores - highest[..., None]), 0.0)
    piece_grads = jnp.einsum(
        "qhe,khe->hqk", short_incoming, fetched_values, preferred_element_type=jnp.float32
    )
    total_sum = piece_weights.sum(axis=-1)
    weighted_sum = (piece_weights * piece_grads).sum(axis=-1)
    short_log_total = highest + jnp.log(total_sum)
    short_dot = weighted_sum / total_sum
    fetched_keys, fetched_values = in_one_piece((short_keys, short_values), SEQ, 0, 1)
    remote_pos = short_order(
        jnp.arange(fetched_keys.shape[0], dtype=jnp.int32), short_rows, group_rows, seq_count
    )
    visible = remote_pos[None, :] <= own_pos[:, None]
    piece_weights = jnp.where(
        visible[None],
        jnp.exp(head_scores(short_queries, fetched_keys) - short_log_total[..., None]),
        0.0,
    )
    piece_grads = jnp.einsum(
        "qhe,khe->hqk", short_incoming, fetched_values, preferred_element_type=jnp.float32
    )
    piece_ds = (piece_weights * (piece_grads - short_dot[..., None])).astype(jnp.bfloat16)
    short_gq = (
        jnp.einsum("hqk,khe->qhe", piece_ds, fetched_keys, preferred_element_type=jnp.float32)
        * temper
    )
    stats_all, dots_all = in_one_piece((short_log_total.T, short_dot.T), SEQ, 0, 1)
    fetched_queries, fetched_incoming = in_one_piece((short_queries, short_incoming), SEQ, 0, 1)
    count = fetched_queries.shape[0]
    remote_pos = short_order(jnp.arange(count, dtype=jnp.int32), short_rows, group_rows, seq_count)
    visible = own_pos[None, :] <= remote_pos[:, None]
    remote_total = stats_all.T
    remote_dot = dots_all.T
    piece_weights = jnp.where(
        visible[None],
        jnp.exp(head_scores(fetched_queries, short_keys) - remote_total[..., None]),
        0.0,
    )
    piece_grads = jnp.einsum(
        "qhe,khe->hqk", fetched_incoming, short_values, preferred_element_type=jnp.float32
    )
    piece_ds = (piece_weights * (piece_grads - remote_dot[..., None])).astype(jnp.bfloat16)
    grad_keys = (
        jnp.einsum("hqk,qhe->khe", piece_ds, fetched_queries, preferred_element_type=jnp.float32)
        * temper
    )
    grad_values = jnp.einsum(
        "hqk,qhe->khe",
        piece_weights.astype(jnp.bfloat16),
        fetched_incoming,
        preferred_element_type=jnp.float32,
    )
    short_gk = grad_keys
    short_gv = grad_values
    short_gq = short_gq.reshape(group_rows, head_width)
    short_gk = short_gk.reshape(group_rows, head_width)
    short_gv = short_gv.reshape(group_rows, head_width)
    grad_pooled_here = (
        grad_here.astype(jnp.float32) + short_gq * gain_query + short_gk * gain_key + short_gv
    )
    empty_width = jnp.zeros((model_width,), jnp.float32)
    grad_short_query = lax.dynamic_update_slice(
        empty_width, jnp.sum(short_gq * pooled_f, axis=0), (group_index * head_width,)
    )
    grad_short_key = lax.dynamic_update_slice(
        empty_width, jnp.sum(short_gk * pooled_f, axis=0), (group_index * head_width,)
    )
    grad_pooled = (
        lax.all_to_all(
            grad_pooled_here.reshape(group_rows, 1, head_width).astype(jnp.bfloat16),
            GRP,
            split_axis=0,
            concat_axis=1,
            tiled=True,
        )
        .astype(jnp.float32)
        .reshape(short_rows, model_width)
    )
    following = shifted_2(grad_pooled[:1], GRP_SEQ, -1)
    grad_following = jnp.concatenate([grad_pooled[1:], following], axis=0)
    spread = jnp.concatenate(
        [
            grad_pooled[:, None],
            jnp.broadcast_to(grad_following[:, None], (short_rows, SHORTEN - 1, model_width)),
        ],
        axis=1,
    ) * (1.0 / SHORTEN)
    grad_mixed = grad_output.astype(jnp.float32) + spread.reshape(local_rows, model_width)
    incoming_heads = grad_mixed.astype(jnp.bfloat16).reshape(local_rows, HEADS, head_size)
    local_dw = jnp.einsum(
        "qhe,khe->hqk", incoming_heads, value_heads, preferred_element_type=jnp.float32
    )
    local_dot = jnp.sum(weights * local_dw, axis=-1, keepdims=True)
    local_ds = (weights * (local_dw - local_dot)).astype(jnp.bfloat16)
    local_gq = (
        jnp.einsum("hqk,khe->qhe", local_ds, key_heads, preferred_element_type=jnp.float32) * temper
    ).reshape(local_rows, model_width)
    full_gk = (
        jnp.einsum("hqk,qhe->khe", local_ds, query_heads, preferred_element_type=jnp.float32)
        * temper
    ).reshape(local_rows + WINDOW, model_width)
    full_gv = jnp.einsum(
        "hqk,qhe->khe", weights_low, incoming_heads, preferred_element_type=jnp.float32
    ).reshape(local_rows + WINDOW, model_width)
    returned = full_gk[:WINDOW] * key_gain + full_gv[:WINDOW]
    arriving = shifted_2(returned.astype(jnp.bfloat16), GRP_SEQ, -1).astype(returned.dtype)
    edge_gain = jnp.sum(full_gk[:WINDOW] * context_f[:WINDOW], axis=0)
    local_gk = full_gk[WINDOW:]
    local_gv = full_gv[WINDOW:]
    grad_tokens = grad_mixed + local_gq * query_gain + local_gk * key_gain + local_gv
    grad_tokens = grad_tokens.at[local_rows - WINDOW :].add(arriving)
    grad_query_gain = jnp.sum(local_gq * token_f, axis=0)
    grad_key_gain = jnp.sum(local_gk * token_f, axis=0) + edge_gain
    summed = one_axis_at_a_time(
        jnp.stack([grad_query_gain, grad_key_gain, grad_short_query, grad_short_key]), GRP_SEQ
    )
    total_tokens = local_rows * lax.axis_size(GRP_SEQ)
    return (grad_tokens.astype(jnp.bfloat16), summed * total_tokens ** (-0.5))


def solution(mesh):
    finer = Mesh(mesh.devices.reshape(2, 8, 4, 4, 2), ("grp_0", "grp_1", "seq_0", "seq_1", "seq_2"))
    return jax.shard_map(
        shards,
        mesh=finer,
        in_specs=(P(GRP_SEQ, None), P(GRP_SEQ, None), P(), P(), P(), P()),
        out_specs=(P(GRP_SEQ, None), P()),
        check_vma=False,
    )
```

profile of v0, /device:TPU:1, one launch (start us, length us, event | category | flops | bytes accessed | tf_op | source)
XLA Modules:
  0.0 362.7 jit_solution(5488367841651119901)
XLA Ops:
  7.2 5.4 %collective-permute-start = (bf16[128,2048]{1,0:T(8,128)(2,1)}, bf16[128,2048]{1,0:T(8,128)(2,1)S(1)}, u32[]{:S(2)}, u32[]{:S(2)}) collective-permute-start(bf16[128,2048]{1,0:T(8,128)(2,1)} %param.10), channel_id=1, source_target_pairs={{0,1},{1,2},{2,3},{3,4},{4,5},{5,6},{6,7},{7,8},{8,9},{9,10},{10,1... | collective-permute-start | bytes 1572872 | tf_op jit(solution)/shard_map/ppermute | solution.py:21
  12.6 2.1 copy.93
  14.6 1.1 fusion.14
  16.3 2.7 collective-permute-done
  19.0 1.0 copy.92
  20.0 2.1 fusion.67
  23.1 1.1 pad_maximum_fusion
  24.2 2.3 copy.67
  26.5 2.8 fusion.24
  29.3 2.7 copy.72
  31.9 1.3 fusion.15
  33.3 4.3 %collective-permute-start.1 = (bf16[15,2048]{1,0:T(8,128)(2,1)S(1)}, bf16[15,2048]{1,0:T(8,128)(2,1)S(1)}, u32[]{:S(2)}, u32[]{:S(2)}) collective-permute-start(bf16[15,2048]{1,0:T(8,128)(2,1)S(1)} %slice.78), channel_id=1, source_target_pairs={{0,1},{1,2},{2,3},{3,4},{4,5},{5,6},{6,7},{7,8},{8,9},{9,10},{10,1... | collective-permute-start | bytes 184328 | tf_op jit(solution)/shard_map/ppermute | solution.py:21
  37.8 1.1 collective-permute-done.1
  39.8 18.8 %all-to-all-start = ((bf16[8,16,256]{2,0,1:T(8,128)(2,1)}), bf16[8,16,256]{2,0,1:T(8,128)(2,1)S(1)}, u32[]{:S(2)}, u32[]{:S(2)}) async-start(bf16[8,16,256]{2,0,1:T(8,128)(2,1)} %pad_maximum_fusion.2), calls=%async_computation | async-start | bytes 131072 | tf_op jit(solution)/shard_map/all_to_all | solution.py:27
  59.5 10.4 %all-to-all-done = bf16[8,16,256]{2,0,1:T(8,128)(2,1)S(1)} async-done(((bf16[8,16,256]{2,0,1:T(8,128)(2,1)}), bf16[8,16,256]{2,0,1:T(8,128)(2,1)S(1)}, u32[]{:S(2)}, u32[]{:S(2)}) %all-to-all-start) | async-done | bytes 65568 | tf_op jit(solution)/shard_map/all_to_all | solution.py:27
  71.4 61.4 %all-gather.3.cloned.1.call-done = bf16[4096,2,128]{2,0,1:T(8,128)(2,1)} async-done(((bf16[128,2,128]{2,0,1:T(8,128)(2,1)}), bf16[4096,2,128]{2,0,1:T(8,128)(2,1)}) %all-gather.3.cloned.1.call-update) | async-done | bytes 2097168 | tf_op jit(solution)/shard_map/all_gather | solution.py:37
  132.8 1.9 fusion.7
  134.7 2.1 fusion.10
  136.9 40.8 %all_gather.12 = f32[4096,2]{0,1:T(2,128)S(1)} all-gather(f32[128,2]{0,1:T(2,128)S(1)} %pad_maximum_fusion.7), channel_id=1, replica_groups=mesh['grp_0'=2,'grp_1'=8,'seq_0'=4,'seq_1'=4,'seq_2'=2] {'seq_0','seq_1'..., dimensions={0}, use_global_device_ids=true | all-gather | bytes 33792 | tf_op jit(solution)/shard_map/all_gather | solution.py:37
  177.7 18.7 %all-gather.5.cloned.1.call-done = bf16[4096,2,128]{2,0,1:T(8,128)(2,1)} async-done(((bf16[128,2,128]{2,0,1:T(8,128)(2,1)}), bf16[4096,2,128]{2,0,1:T(8,128)(2,1)}) %all-gather.5.cloned.1.call-update) | async-done | bytes 2097168 | tf_op jit(solution)/shard_map/all_gather | solution.py:37
  196.4 3.3 fusion.3
  199.6 3.5 fusion.12
  203.1 3.4 fusion.28
  208.6 21.5 %all_to_all.27 = bf16[16,2,512]{2,1,0:T(2,128)(2,1)S(1)} all-to-all(bf16[16,2,512]{2,1,0:T(2,128)(2,1)S(1)} %reshape.635), channel_id=1, replica_groups=mesh['grp_0'=2,'grp_1'=8,'seq_0'=4,'seq_1'=4,'seq_2'=2] {'grp_0','grp_1'}, dimensions={0} | all-to-all | bytes 65536 | tf_op jit(solution)/shard_map/all_to_all | solution.py:213
  230.2 3.8 %collective-permute-start.2 = (f32[1,2048]{1,0:T(1,128)S(1)}, f32[1,2048]{1,0:T(1,128)S(1)}, u32[]{:S(2)}, u32[]{:S(2)}) collective-permute-start(f32[1,2048]{1,0:T(1,128)S(1)} %slice_bitcast_fusion.13), channel_id=1, source_target_pairs={{1,0},{2,1},{3,2},{4,3},{5,4},{6,5},{7,6},{8,7},{9,8},{10,9},{11,1... | collective-permute-start | bytes 24584 | tf_op jit(solution)/shard_map/ppermute | solution.py:21
  234.0 1.5 collective-permute-done.2
  235.9 1.0 copy-done.1
  237.8 2.0 copy.95
  239.8 1.7 convolution_bitcast_fusion
  241.5 2.2 multiply_reduce_fusion
  243.8 1.6 fusion.64
  245.4 2.6 copy.85
  248.0 2.0 multiply_convert_fusion
  250.0 1.0 copy-done.10
  251.4 1.6 fusion.63
  253.1 2.7 copy.84
  255.8 2.3 multiply_reduce_fusion.2
  258.0 2.0 collective-permute-start.3
  260.2 2.7 copy.83
  262.8 1.3 copy.81
  264.2 2.8 convolution_multiply_fusion.2
  266.9 2.6 copy.79
  269.6 3.0 fusion.16
  272.6 12.9 %psum.35 = f32[4,2048]{1,0:T(4,128)S(1)} all-reduce(f32[4,2048]{1,0:T(4,128)S(1)} %pad_maximum_fusion.6), channel_id=1, replica_groups=mesh['grp_0'=2,'grp_1'=8,'seq_0'=4,'seq_1'=4,'seq_2'=2] {'grp_0'}, use_global_device_ids=true, to_apply=%region_13.14 | all-reduce | flops 8192 | bytes 65536 | tf_op jit(solution)/shard_map/psum | solution.py:42
  285.5 20.4 %psum.36 = f32[4,2048]{1,0:T(4,128)S(1)} all-reduce(f32[4,2048]{1,0:T(4,128)S(1)} %psum.35), channel_id=1, replica_groups=mesh['grp_0'=2,'grp_1'=8,'seq_0'=4,'seq_1'=4,'seq_2'=2] {'grp_1'}, use_global_device_ids=true, to_apply=%region_14.15 | all-reduce | flops 8192 | bytes 65536 | tf_op jit(solution)/shard_map/psum | solution.py:42
  305.9 10.9 %psum.37 = f32[4,2048]{1,0:T(4,128)S(1)} all-reduce(f32[4,2048]{1,0:T(4,128)S(1)} %psum.36), channel_id=1, replica_groups=mesh['grp_0'=2,'grp_1'=8,'seq_0'=4,'seq_1'=4,'seq_2'=2] {'seq_0'}, use_global_device_ids=true, to_apply=%region_15.16 | all-reduce | flops 8192 | bytes 65536 | tf_op jit(solution)/shard_map/psum | solution.py:42
  316.9 21.4 %psum.38 = f32[4,2048]{1,0:T(4,128)S(1)} all-reduce(f32[4,2048]{1,0:T(4,128)S(1)} %psum.37), channel_id=1, replica_groups=mesh['grp_0'=2,'grp_1'=8,'seq_0'=4,'seq_1'=4,'seq_2'=2] {'seq_1'}, use_global_device_ids=true, to_apply=%region_16.17 | all-reduce | flops 8192 | bytes 65536 | tf_op jit(solution)/shard_map/psum | solution.py:42
  338.3 16.9 %psum.39 = f32[4,2048]{1,0:T(4,128)S(1)} all-reduce(f32[4,2048]{1,0:T(4,128)S(1)} %psum.38), channel_id=1, replica_groups=mesh['grp_0'=2,'grp_1'=8,'seq_0'=4,'seq_1'=4,'seq_2'=2] {'seq_2'}, use_global_device_ids=true, to_apply=%region_17.18 | all-reduce | flops 8192 | bytes 65536 | tf_op jit(solution)/shard_map/psum | solution.py:42
  (90 shorter events, 9.3 us)
Async XLA Ops:
  7.2 11.8 %collective-permute-start = (bf16[128,2048]{1,0:T(8,128)(2,1)}, bf16[128,2048]{1,0:T(8,128)(2,1)S(1)}, u32[]{:S(2)}, u32[]{:S(2)}) collective-permute-start(bf16[128,2048]{1,0:T(8,128)(2,1)} %param.10), channel_id=1, source_target_pairs={{0,1},{1,2},{2,3},{3,4},{4,5},{5,6},{6,7},{7,8},{8,9},{9,10},{10,1... | collective-permute-start | bytes 1572872 | tf_op jit(solution)/shard_map/ppermute | solution.py:21
  12.6 7.4 %copy-start.20 = (f32[2048]{0:T(1024)S(1)}, f32[2048]{0:T(1024)}, u32[]{:S(2)}) copy-start(f32[2048]{0:T(1024)} %param.13) | copy-start | bytes 24580
  16.1 3.9 %copy-start.15 = (bf16[128,2048]{0,1:T(8,128)(2,1)}, bf16[128,2048]{0,1:T(8,128)(2,1)S(1)}, u32[]{:S(2)}) copy-start(bf16[128,2048]{0,1:T(8,128)(2,1)S(1)} %copy.94) | copy-start | bytes 1572868
  19.0 3.8 %copy-start.7 = (bf16[128,2048]{1,0:T(8,128)(2,1)}, bf16[128,2048]{1,0:T(8,128)(2,1)S(1)}, u32[]{:S(2)}) copy-start(bf16[128,2048]{1,0:T(8,128)(2,1)S(1)} %collective-permute-done) | copy-start | bytes 1572868
  22.1 1.0 copy-start
  29.3 8.3 %copy-start.6 = (bf16[128,2048]{1,0:T(8,128)(2,1)S(1)}, bf16[128,2048]{1,0:T(8,128)(2,1)}, u32[]{:S(2)}) copy-start(bf16[128,2048]{1,0:T(8,128)(2,1)} %param.11) | copy-start | bytes 1572868
  33.3 5.6 %collective-permute-start.1 = (bf16[15,2048]{1,0:T(8,128)(2,1)S(1)}, bf16[15,2048]{1,0:T(8,128)(2,1)S(1)}, u32[]{:S(2)}, u32[]{:S(2)}) collective-permute-start(bf16[15,2048]{1,0:T(8,128)(2,1)S(1)} %slice.78), channel_id=1, source_target_pairs={{0,1},{1,2},{2,3},{3,4},{4,5},{5,6},{6,7},{7,8},{8,9},{9,10},{10,1... | collective-permute-start | bytes 184328 | tf_op jit(solution)/shard_map/ppermute | solution.py:21
  39.8 30.1 %all-to-all-start = ((bf16[8,16,256]{2,0,1:T(8,128)(2,1)}), bf16[8,16,256]{2,0,1:T(8,128)(2,1)S(1)}, u32[]{:S(2)}, u32[]{:S(2)}) async-start(bf16[8,16,256]{2,0,1:T(8,128)(2,1)} %pad_maximum_fusion.2), calls=%async_computation | async-start | bytes 131072 | tf_op jit(solution)/shard_map/all_to_all | solution.py:27
  58.6 74.2 %all-gather.3.cloned.1.call-start = ((), (), s32[]{:S(2)}) async-start(), calls=%async_computation.2 | async-start | bytes 2162688 | tf_op jit(solution)/shard_map/all_gather | solution.py:37
  70.6 125.8 %all-gather.5.cloned.1.call-start = ((), (), s32[]{:S(2)}) async-start(), calls=%async_computation.3 | async-start | bytes 2162688 | tf_op jit(solution)/shard_map/all_gather | solution.py:37
  132.8 1.9 copy-start.18
  134.7 2.2 copy-start.17
  203.1 3.5 copy-start.4
  203.1 3.8 %copy-start.5 = (bf16[4096,2,128]{2,0,1:T(8,128)(2,1)S(1)}, bf16[4096,2,128]{2,0,1:T(8,128)(2,1)}, u32[]{:S(2)}) copy-start(bf16[4096,2,128]{2,0,1:T(8,128)(2,1)} %all-gather.5.cloned.1.call-done) | copy-start | bytes 6291460
  230.2 5.4 %collective-permute-start.2 = (f32[1,2048]{1,0:T(1,128)S(1)}, f32[1,2048]{1,0:T(1,128)S(1)}, u32[]{:S(2)}, u32[]{:S(2)}) collective-permute-start(f32[1,2048]{1,0:T(1,128)S(1)} %slice_bitcast_fusion.13), channel_id=1, source_target_pairs={{1,0},{2,1},{3,2},{4,3},{5,4},{6,5},{7,6},{8,7},{9,8},{10,9},{11,1... | collective-permute-start | bytes 24584 | tf_op jit(solution)/shard_map/ppermute | solution.py:21
  235.8 1.0 copy-start.1
  239.8 1.7 copy-start.3
  239.8 1.7 copy-start.9
  248.0 3.0 copy-start.16
  250.0 1.0 copy-start.10
  253.1 2.7 copy-start.8
  253.1 2.7 copy-start.12
  258.0 4.8 %copy-start.13 = (f32[128,16,128]{0,2,1:T(8,128)S(1)}, f32[128,16,128]{0,2,1:T(8,128)}, u32[]{:S(2)}) copy-start(f32[128,16,128]{0,2,1:T(8,128)} %get-tuple-element.33) | copy-start | bytes 3145732
  258.0 11.5 %collective-permute-start.3 = (bf16[128,2048]{1,0:T(8,128)(2,1)}, bf16[128,2048]{1,0:T(8,128)(2,1)}, u32[]{:S(2)}, u32[]{:S(2)}) collective-permute-start(bf16[128,2048]{1,0:T(8,128)(2,1)} %get-tuple-element.38), channel_id=1, source_target_pairs={{1,0},{2,1},{3,2},{4,3},{5,4},{6,5},{7,6},{8,7},{9,8},{10,9},{11,1... | collective-permute-start | bytes 1572872 | tf_op jit(solution)/shard_map/ppermute | solution.py:21
  260.1 4.0 %copy-start.11 = (bf16[16,128,256]{2,1,0:T(8,128)(2,1)S(1)}, bf16[16,128,256]{2,1,0:T(8,128)(2,1)}, u32[]{:S(2)}) copy-start(bf16[16,128,256]{2,1,0:T(8,128)(2,1)} %copy-done.10) | copy-start | bytes 3145732
  264.2 5.4 %copy-start.2 = (f32[8,16,2048]{2,1,0:T(8,128)S(1)}, f32[8,16,2048]{2,1,0:T(8,128)}, u32[]{:S(2)}) copy-start(f32[8,16,2048]{2,1,0:T(8,128)} %copy-done.1) | copy-start | bytes 3145732
  264.2 5.4 %copy-start.19 = (f32[2048]{0:T(1024)S(1)}, f32[2048]{0:T(1024)}, u32[]{:S(2)}) copy-start(f32[2048]{0:T(1024)} %param.12) | copy-start | bytes 24580
  266.9 2.7 copy-start.14
Sparse Core Ops, SparseCore 0:
  70.7 62.0 all-gather.2
  134.9 61.3 all-gather.4
where the time goes:
time: 364 us; the launch traced here: 363 us
  blocking collectives  145 us (40%)
  waiting for transfers between devices  96 us (26%)
  starting transfers between devices  34.4 us (9%)
  local copies, waits for them, and re-layouts  29 us (8%)
  matrix products  26.7 us (7%)
  other arithmetic  17.2 us (5%)
  between operations  14.6 us (4%)
    psum x5, blocking collectives, one_axis_at_a_time(): x = lax.psum(x, axis)  82.5 us
    all_gather x2, waiting for transfers between devices, in_one_piece(): lax.all_gather(both, axis, axis=dim, tiled=True)  80.1 us
    all_gather x1, blocking collectives, in_one_piece(): lax.all_gather(both, axis, axis=dim, tiled=True)  40.8 us
    all_to_all x1, blocking collectives, shards(): lax.all_to_all(grad_pooled_here.reshape(group_rows, 1, head_width).astype...  21.5 us
    all_to_all x1, starting transfers between devices, side_by_side(): lax.all_to_all(both, axis, split_axis=split_dim, concat_axis=concat_dim,...  18.8 us
    ppermute x4, starting transfers between devices, shifted_2(): lax.ppermute(value, axis, [(source, source + steps) for source in range(l...  15.5 us
    all_to_all x1, waiting for transfers between devices, side_by_side(): lax.all_to_all(both, axis, split_axis=split_dim, concat_axis=concat_dim,...  10.4 us
  transfers between devices with their start and end apart: 7, of which 6 were waited for; matrix products, arithmetic and copies ran while one was open for 5% of the time, Pallas kernels for 0%

commit v1 on v0

v1 whole, which is shorter than its diff:
```python
import functools

import jax
import jax.numpy as jnp
from jax import lax
from jax.experimental import pallas as pl
from jax.experimental.pallas import tpu as pltpu
from jax.sharding import Mesh
from jax.sharding import PartitionSpec as P

AXES = ("zh", "y", "x", "zl", "c")
MESH = pl.DeviceIdType.MESH
T = 128
HD = 128
SLOTS = 8
NEGATIVE = -1e30
TEMPER = HD ** (-0.5)
F32 = jnp.float32
BF16 = jnp.bfloat16
GROUP = 4


def mm(a, b):
    return jnp.dot(a, b, preferred_element_type=F32)


def mm_nt(a, b):
    return lax.dot_general(a, b, (((1,), (1,)), ((), ())), preferred_element_type=F32)


def mm_tn(a, b):
    return lax.dot_general(a, b, (((0,), (0,)), ((), ())), preferred_element_type=F32)


def iota(shape, dim):
    return lax.broadcasted_iota(jnp.int32, shape, dim)


def remote(src, dst, send, recv, device):
    return pltpu.make_async_remote_copy(
        src_ref=src, dst_ref=dst, send_sem=send, recv_sem=recv, device_id=device, device_id_type=MESH
    )


def loop(count, body, start=0):
    def step(k, carry):
        body(k)
        return carry

    lax.fori_loop(start, count, step, 0)


def kernel(
    sizes,
    tok, gout, qg, kg, sqg, skg,
    out, gains,
    ctx, gsrc, tnext, wt, pg_send, pg_recv, pgx, kz, prob, dprob, dk, dv, stats,
    qgr_send, qgr_recv, kgr_send, kgr_recv, gp_send, gp_recv, gp_prev,
    ret_send, ret_recv, acc, outv, gr_send, gr_recv, gx, gz, gfin,
    load_sem, next_send, next_recv, tok_send, tok_recv, a_send, a_recv, x_send, x_recv, z_send, z_recv,
    prev_send, prev_recv,
):
    nzh, ny, nx, nzl, nc = sizes
    nz, na = nzh * nzl, ny * nc
    heads = na
    span = na * SLOTS
    zh, y, x, zl, c = [lax.axis_index(name) for name in AXES]
    z = zh * nzl + zl
    a = y * nc + c
    chain = (((zh * ny + y) * nx + x) * nzl + zl) * nc + c
    total = nzh * ny * nx * nzl * nc

    def decode(index):
        return (
            index // (ny * nx * nzl * nc),
            index // (nx * nzl * nc) % ny,
            index // (nzl * nc) % nx,
            index // nc % nzl,
            index % nc,
        )

    following = decode((chain + 1) % total)
    previous = decode((chain + total - 1) % total)

    def at_a(other):
        return (zh, other // nc, x, zl, other % nc)

    def at_x(other):
        return (zh, y, other, zl, c)

    def at_z(other):
        return (other // nzl, y, x, other % nzl, c)

    barrier = pltpu.get_barrier_semaphore()

    def greet(device):
        pl.semaphore_signal(barrier, inc=1, device_id=device, device_id_type=MESH)

    greet(following)
    greet(previous)
    loop(na, lambda k: greet(at_a((a + k) % na)), 1)
    loop(nz, lambda k: greet(at_z((z + k) % nz)), 1)
    loop(nx, lambda k: greet(at_x((x + k) % nx)), 1)

    load_tok = pltpu.make_async_copy(tok, ctx.at[pl.ds(T, T)], load_sem.at[0])
    load_gout = pltpu.make_async_copy(gout, gsrc.at[pl.ds(0, T)], load_sem.at[1])
    load_tok.start()
    load_gout.start()

    pl.semaphore_wait(barrier, 2 + (na - 1) + (nz - 1) + (nx - 1))

    def columns(h):
        return pl.ds(pl.multiple_of(h * HD, HD), HD)

    head_tok = remote(tok.at[pl.ds(0, 16)], tnext, next_send.at[0], next_recv.at[0], previous)
    head_gout = remote(gout.at[pl.ds(0, 16)], gsrc.at[pl.ds(T, 16)], next_send.at[1], next_recv.at[1], previous)
    head_tok.start()
    head_gout.start()

    def tokens_of(h):
        return remote(
            tok.at[:, columns(h)], ctx.at[pl.ds(0, T), columns(h)], tok_send.at[h], tok_recv.at[h], following
        )

    loop(heads, lambda h: tokens_of(h).start())

    load_tok.wait()
    load_gout.wait()
    head_tok.wait_recv()
    head_gout.wait_recv()

    key_row = iota((T, T), 0)
    query_col = iota((T, T), 1)
    prior = key_row > query_col
    first_bias = jnp.where(chain == 0, NEGATIVE, 0.0)
    last_bias = jnp.where(chain == total - 1, NEGATIVE, 0.0)
    not_last = jnp.where(chain == total - 1, 0.0, 1.0)
    top_row = iota((T, HD), 0) == 0
    ext_bias = jnp.where(iota((T, 16), 0) == 0, 0.0, last_bias)
    slot = iota((SLOTS, T), 0)
    row = iota((SLOTS, T), 1)
    keep = jnp.where(slot == SLOTS - 1, not_last, 1.0)
    pool = jnp.where((row > slot * 16) & (row <= slot * 16 + 16), keep, 0.0).astype(BF16)
    gpool = jnp.where((row >= slot * 16 + 16) & (row < slot * 16 + 32), 1.0, 0.0).astype(BF16)
    tail = iota((SLOTS, HD), 0) == SLOTS - 1

    def exchange(kind, h):
        send, recv, ssem, rsem = kind
        return remote(send.at[h], recv.at[a], ssem.at[h], rsem.at[a], at_a(h))

    def arrived(kind, h):
        send, recv, ssem, rsem = kind
        remote(send.at[h], recv.at[h], ssem.at[h], rsem.at[h], at_a(h)).wait_recv()

    def others_a(body):
        loop(na, lambda k: body((a + k) % na), 1)

    pg_kind = (pg_send, pg_recv, a_send.at[0], a_recv.at[0])
    gp_kind = (gp_send, gp_recv, a_send.at[1], a_recv.at[1])
    gr_kind = (gr_send, gr_recv, a_send.at[2], a_recv.at[2])

    def forward(h):
        cols = columns(h)
        both = ctx[:, cols]
        both_f = both.astype(F32)
        own_f = both_f[T:]
        gq, gk = qg[:, cols], kg[:, cols]
        queries = (own_f * gq).astype(BF16)
        keys = (both_f * gk).astype(BF16)
        scores = mm_nt(keys, queries) * TEMPER
        scores = jnp.where(prior, scores[:T] + first_bias, scores[T:])
        weights = jnp.exp(scores - scores.max(axis=0, keepdims=True))
        weights = weights * (1.0 / weights.sum(axis=0, keepdims=True))
        wt[h] = weights
        split = jnp.concatenate([jnp.where(prior, weights, 0.0), jnp.where(prior, 0.0, weights)], axis=0)
        mixed = (own_f + mm_tn(split.astype(BF16), both)).astype(BF16)
        ext_f = tnext[:, cols].astype(F32)
        ext_values = jnp.where(top_row, ext_f[0:1], own_f)
        ext_queries = (ext_f * gq).astype(BF16)
        ext_keys = (ext_values * gk).astype(BF16)
        ext_scores = mm_nt(ext_keys, ext_queries) * TEMPER + ext_bias
        ext_weights = jnp.exp(ext_scores - ext_scores.max(axis=0, keepdims=True))
        ext_weights = ext_weights * (1.0 / ext_weights.sum(axis=0, keepdims=True))
        ext_mixed = (ext_f + mm_tn(ext_weights.astype(BF16), ext_values.astype(BF16))).astype(BF16)
        pooled = mm(pool, mixed) + jnp.where(tail, ext_mixed.astype(F32)[0:1], 0.0)
        incoming = gsrc[pl.ds(0, T), cols]
        short = mm(gpool, incoming)
        next_sum = gsrc[pl.ds(T, 16), cols].astype(F32).sum(axis=0, keepdims=True)
        short = short + jnp.where(tail, next_sum, 0.0)
        pg_send[h] = jnp.concatenate([pooled * (1.0 / 16), short], axis=0).astype(BF16)

        @pl.when(h != a)
        def _():
            exchange(pg_kind, h).start()

        @pl.when(h == a)
        def _():
            pg_recv[h] = pg_send[h]

    def forward_group(g):
        for u in range(GROUP):
            tokens_of(g * GROUP + u).wait_recv()
        for u in range(GROUP):
            forward(g * GROUP + u)

    loop(heads // GROUP, forward_group)
    others_a(lambda h: arrived(pg_kind, h))

    blocks = pg_recv[...].astype(F32)
    pooled_own = blocks[:, :SLOTS].reshape(span, HD).astype(BF16)
    short_own = blocks[:, SLOTS:].reshape(span, HD)
    pgx[x, 0] = pooled_own
    pgx[x, 1] = short_own.astype(BF16)
    kz[z] = pooled_own

    def gather_x(other):
        return remote(pgx.at[x], pgx.at[x], x_send.at[0, other], x_recv.at[0, x], at_x(other))

    def gather_z(other):
        return remote(kz.at[z], kz.at[z], z_send.at[0, other], z_recv.at[0, z], at_z(other))

    def others_x(body):
        loop(nx, lambda k: body((x + k) % nx), 1)

    def others_z(body):
        loop(nz, lambda k: body((z + k) % nz), 1)

    others_z(lambda o: gather_z(o).start())
    others_x(lambda o: gather_x(o).start())

    def x_arrived(phase, ref, other):
        remote(ref.at[other], ref.at[other], x_send.at[phase, other], x_recv.at[phase, other], at_x(other)).wait_recv()

    def z_arrived(phase, ref, other):
        remote(ref.at[other], ref.at[other], z_send.at[phase, other], z_recv.at[phase, other], at_z(other)).wait_recv()

    def position(zi, xi, index):
        source, place = index // SLOTS, index % SLOTS
        device = ((zi // nzl * ny + source // nc) * nx + xi) * nzl * nc + zi % nzl * nc + source % nc
        raw = device * SLOTS + place + 1
        return jnp.where(raw == total * SLOTS, 0, raw)

    head_cols = columns(a)
    gain_query = sqg[:, head_cols]
    gain_key = skg[:, head_cols]

    others_z(lambda o: z_arrived(0, kz, o))
    others_x(lambda o: x_arrived(0, pgx, o))

    count = nz * span
    values = kz[...].reshape(count, HD)
    short_keys = (values.astype(F32) * gain_key).astype(BF16)
    key_index = iota((count, 1), 0)
    key_pos = position(key_index // span, x, key_index % span)

    def first_pass(b):
        queries = (pgx[b, 0].astype(F32) * gain_query).astype(BF16)
        query_pos = position(z, b, iota((1, span), 1))
        visible = key_pos <= query_pos
        scores = jnp.where(visible, mm_nt(short_keys, queries) * TEMPER, NEGATIVE)
        highest = jnp.maximum(scores.max(axis=0, keepdims=True), 0.1 * NEGATIVE)
        weights = jnp.exp(scores - highest)
        grads = mm_nt(values, pgx[b, 1])
        prob[b] = weights
        dprob[b] = grads
        sums = weights.sum(axis=0, keepdims=True)
        dots = (weights * grads).sum(axis=0, keepdims=True)
        stats[x, b] = jnp.concatenate([highest, sums, dots, jnp.zeros((5, span), F32)], axis=0)

    loop(nx, first_pass)

    def send_stats(other):
        return remote(stats.at[x], stats.at[x], x_send.at[1, other], x_recv.at[1, x], at_x(other))

    others_x(lambda o: send_stats(o).start())
    dk[...] = jnp.zeros_like(dk)
    dv[...] = jnp.zeros_like(dv)
    others_x(lambda o: x_arrived(1, stats, o))

    def send_query(other):
        return remote(qgr_send.at[other], qgr_recv.at[x], x_send.at[2, other], x_recv.at[2, x], at_x(other))

    def send_key(other):
        return remote(kgr_send.at[other], kgr_recv.at[z], z_send.at[1, other], z_recv.at[1, z], at_z(other))

    gr_short = jnp.zeros((1, HD), F32)

    def second_pass(b, gain_sum):
        pieces = [stats[s, b] for s in range(nx)]
        top = pieces[0][0:1]
        for piece in pieces[1:]:
            top = jnp.maximum(top, piece[0:1])
        sums = jnp.zeros((1, span), F32)
        dots = jnp.zeros((1, span), F32)
        for piece in pieces:
            factor = jnp.exp(piece[0:1] - top)
            sums = sums + piece[1:2] * factor
            dots = dots + piece[2:3] * factor
        inverse = 1.0 / sums
        mine = jnp.exp(stats[x, b][0:1] - top) * inverse
        dots = dots * inverse
        weights = prob[b] * mine
        ds = (weights * (dprob[b] - dots)).astype(BF16)
        pooled_f = pgx[b, 0].astype(F32)
        queries = (pooled_f * gain_query).astype(BF16)
        dk[...] += mm(ds, queries)
        dv[...] += mm(weights.astype(BF16), pgx[b, 1])
        grad_q = mm_tn(ds, short_keys) * TEMPER
        qgr_send[b] = (grad_q * gain_query).astype(BF16)

        @pl.when(b != x)
        def _():
            send_query(b).start()

        @pl.when(b == x)
        def _():
            qgr_recv[b] = qgr_send[b]

        return gain_sum + (grad_q * pooled_f).sum(axis=0, keepdims=True)

    gain_short_query = lax.fori_loop(0, nx, second_pass, gr_short)
    grad_k = dk[...] * TEMPER
    gain_short_key = (grad_k * values.astype(F32)).sum(axis=0, keepdims=True)
    kgr_send[...] = (grad_k * gain_key + dv[...]).astype(BF16).reshape(nz, span, HD)
    others_z(lambda o: send_key(o).start())
    kgr_recv[z] = kgr_send[z]
    others_x(lambda o: x_arrived(2, qgr_recv, o))
    others_z(lambda o: z_arrived(1, kgr_recv, o))
    grad_pooled = short_own + qgr_recv[...].astype(F32).sum(axis=0) + kgr_recv[...].astype(F32).sum(axis=0)
    gp_send[...] = grad_pooled.reshape(na, SLOTS, HD)
    others_a(lambda h: exchange(gp_kind, h).start())
    gp_recv[a] = gp_send[a]
    others_a(lambda h: arrived(gp_kind, h))
    pass_on = remote(gp_recv, gp_prev, next_send.at[2], next_recv.at[2], following)
    pass_on.start()
    pass_on.wait_recv()

    token = iota((T, 16), 0)
    place = iota((T, 16), 1)
    source = jnp.where(token == 0, 15, (token + 15) // 16 - 1)
    spread = jnp.where(place == source, jnp.where(place == SLOTS - 1, not_last, 1.0) * (1.0 / 16), 0.0).astype(BF16)

    def give_back(h):
        return remote(ret_send.at[h], ret_recv.at[h], prev_send.at[h], prev_recv.at[h], previous)

    def backward(h):
        cols = columns(h)
        both = ctx[:, cols]
        both_f = both.astype(F32)
        own_f = both_f[T:]
        gq, gk = qg[:, cols], kg[:, cols]
        queries = (own_f * gq).astype(BF16)
        keys = (both_f * gk).astype(BF16)
        rows = jnp.concatenate([gp_recv[h], gp_prev[h]], axis=0).astype(BF16)
        grad_mixed = gsrc[pl.ds(0, T), cols].astype(F32) + mm(spread, rows)
        incoming = grad_mixed.astype(BF16)
        grads = mm_nt(both, incoming)
        grads = jnp.where(prior, grads[:T], grads[T:])
        weights = wt[h]
        dots = (weights * grads).sum(axis=0, keepdims=True)
        ds = weights * (grads - dots)
        ds = jnp.concatenate([jnp.where(prior, ds, 0.0), jnp.where(prior, 0.0, ds)], axis=0).astype(BF16)
        split = jnp.concatenate([jnp.where(prior, weights, 0.0), jnp.where(prior, 0.0, weights)], axis=0).astype(BF16)
        grad_q = mm_tn(ds, keys) * TEMPER
        grad_k = mm(ds, queries) * TEMPER
        to_keys = grad_k * gk + mm(split, incoming)
        ret_send[h] = to_keys[:T].astype(BF16)
        give_back(h).start()
        acc[h] = grad_mixed + grad_q * gq + to_keys[T:]
        sum_q = (grad_q * own_f).sum(axis=0, keepdims=True)
        sum_k = (grad_k * both_f).sum(axis=0, keepdims=True)
        gr_send[h] = jnp.concatenate([sum_q, sum_k, jnp.zeros((6, HD), F32)], axis=0)

        @pl.when(h != a)
        def _():
            exchange(gr_kind, h).start()

        @pl.when(h == a)
        def _():
            gr_recv[h] = gr_send[h]

    def backward_group(g):
        for u in range(GROUP):
            backward(g * GROUP + u)

    loop(heads // GROUP, backward_group)

    def finish(h):
        give_back(h).wait_recv()
        outv[:, columns(h)] = (acc[h] + ret_recv[h].astype(F32)).astype(BF16)

    loop(heads, finish)
    store = pltpu.make_async_copy(outv, out, load_sem.at[2])
    store.start()

    others_a(lambda h: arrived(gr_kind, h))
    short_rows = jnp.concatenate([jnp.zeros((2, HD), F32), gain_short_query, gain_short_key, jnp.zeros((4, HD), F32)], axis=0)
    gx[x] = gr_recv[...].sum(axis=0) + short_rows

    def sum_x(other):
        return remote(gx.at[x], gx.at[x], x_send.at[3, other], x_recv.at[3, x], at_x(other))

    def sum_z(other):
        return remote(gz.at[z], gz.at[z], z_send.at[2, other], z_recv.at[2, z], at_z(other))

    def share(other):
        return remote(gfin.at[a], gfin.at[a], a_send.at[3, other], a_recv.at[3, a], at_a(other))

    others_x(lambda o: sum_x(o).start())
    others_x(lambda o: x_arrived(3, gx, o))
    gz[z] = gx[...].sum(axis=0)
    others_z(lambda o: sum_z(o).start())
    others_z(lambda o: z_arrived(2, gz, o))
    gfin[a] = gz[...].sum(axis=0) * (float(total * T) ** (-0.5))
    others_a(lambda h: share(h).start())
    others_a(
        lambda h: remote(gfin.at[h], gfin.at[h], a_send.at[3, h], a_recv.at[3, h], at_a(h)).wait_recv()
    )

    def put(h):
        gains[:, columns(h)] = gfin[h][0:4]

    loop(heads, put)

    head_tok.wait_send()
    head_gout.wait_send()
    pass_on.wait_send()

    def drain(h):
        tokens_of(h).wait_send()
        give_back(h).wait_send()

    loop(heads, drain)

    def drain_a(h):
        exchange(pg_kind, h).wait_send()
        exchange(gp_kind, h).wait_send()
        exchange(gr_kind, h).wait_send()
        share(h).wait_send()

    others_a(drain_a)

    def drain_x(o):
        gather_x(o).wait_send()
        send_stats(o).wait_send()
        send_query(o).wait_send()
        sum_x(o).wait_send()

    others_x(drain_x)

    def drain_z(o):
        gather_z(o).wait_send()
        send_key(o).wait_send()
        sum_z(o).wait_send()

    others_z(drain_z)
    store.wait()


def shards(sizes, tokens, grad_output, query_gain, key_gain, short_query_gain, short_key_gain):
    nzh, ny, nx, nzl, nc = sizes
    nz, na = nzh * nzl, ny * nc
    width = tokens.shape[1]
    heads = width // HD
    span = na * SLOTS
    vmem = pl.BlockSpec(memory_space=pltpu.VMEM)
    hbm = pl.BlockSpec(memory_space=pl.ANY)
    dma = pltpu.SemaphoreType.DMA
    scratch = [
        pltpu.VMEM((2 * T, width), BF16),
        pltpu.VMEM((T + 16, width), BF16),
        pltpu.VMEM((16, width), BF16),
        pltpu.VMEM((heads, T, T), F32),
        pltpu.VMEM((na, 16, HD), BF16),
        pltpu.VMEM((na, 16, HD), BF16),
        pltpu.VMEM((nx, 2, span, HD), BF16),
        pltpu.VMEM((nz, span, HD), BF16),
        pltpu.VMEM((nx, nz * span, span), F32),
        pltpu.VMEM((nx, nz * span, span), F32),
        pltpu.VMEM((nz * span, HD), F32),
        pltpu.VMEM((nz * span, HD), F32),
        pltpu.VMEM((nx, nx, 8, span), F32),
        pltpu.VMEM((nx, span, HD), BF16),
        pltpu.VMEM((nx, span, HD), BF16),
        pltpu.VMEM((nz, span, HD), BF16),
        pltpu.VMEM((nz, span, HD), BF16),
        pltpu.VMEM((na, SLOTS, HD), F32),
        pltpu.VMEM((na, SLOTS, HD), F32),
        pltpu.VMEM((na, SLOTS, HD), F32),
        pltpu.VMEM((heads, T, HD), BF16),
        pltpu.VMEM((heads, T, HD), BF16),
        pltpu.VMEM((heads, T, HD), F32),
        pltpu.VMEM((T, width), BF16),
        pltpu.VMEM((na, 8, HD), F32),
        pltpu.VMEM((na, 8, HD), F32),
        pltpu.VMEM((nx, 8, HD), F32),
        pltpu.VMEM((nz, 8, HD), F32),
        pltpu.VMEM((na, 8, HD), F32),
        dma((3,)),
        dma((3,)),
        dma((3,)),
        dma((heads,)),
        dma((heads,)),
        dma((4, na)),
        dma((4, na)),
        dma((4, nx)),
        dma((4, nx)),
        dma((3, nz)),
        dma((3, nz)),
        dma((heads,)),
        dma((heads,)),
    ]
    return pl.pallas_call(
        functools.partial(kernel, sizes),
        out_shape=(
            jax.ShapeDtypeStruct(tokens.shape, BF16),
            jax.ShapeDtypeStruct((4, width), F32),
        ),
        in_specs=[hbm, hbm, vmem, vmem, vmem, vmem],
        out_specs=(hbm, vmem),
        scratch_shapes=scratch,
        compiler_params=pltpu.CompilerParams(collective_id=0, has_side_effects=True),
        name="hourglass",
    )(
        tokens,
        grad_output,
        query_gain.reshape(1, width),
        key_gain.reshape(1, width),
        short_query_gain.reshape(1, width),
        short_key_gain.reshape(1, width),
    )


def build(mesh, sizes):
    finer = Mesh(mesh.devices.reshape(sizes), AXES)
    return jax.shard_map(
        functools.partial(shards, sizes),
        mesh=finer,
        in_specs=(P(AXES, None), P(AXES, None), P(), P(), P(), P()),
        out_specs=(P(AXES, None), P()),
        check_vma=False,
    )


def solution(mesh):
    return build(mesh, (2, 8, 4, 4, 2))
```

time: 364 us -> 104 us (0.29)
  blocking collectives: 145 us -> 0 us
  Pallas kernels: 0 us -> 101 us
  waiting for transfers between devices: 96 us -> 0 us
  starting transfers between devices: 34.4 us -> 0 us
  matrix products: 26.7 us -> 0 us
  local copies, waits for them, and re-layouts: 29 us -> 2.51 us
  other arithmetic: 17.2 us -> 0 us
  between operations: 14.6 us -> 0.65 us
    pallas_call x0 -> x1, Pallas kernels: none -> 101 us  [shards(): pl.pallas_call(functools.partial(kernel, sizes), out_shape=(jax.ShapeDtyp...]
    psum x5 -> x0, blocking collectives: 82.5 us -> none  [one_axis_at_a_time(): x = lax.psum(x, axis)]
    all_gather x2 -> x0, waiting for transfers between devices: 80.1 us -> none  [in_one_piece(): lax.all_gather(both, axis, axis=dim, tiled=True)]
    all_gather x1 -> x0, blocking collectives: 40.8 us -> none  [in_one_piece(): lax.all_gather(both, axis, axis=dim, tiled=True)]
    dot_general x12 -> x0, matrix products: 26.7 us -> none  [the longest x3 7.27 us: head_scores(): jnp.einsum('qhe,khe->hqk', queries, key_rows, preferred_element_type=jnp....]
    all_to_all x1 -> x0, blocking collectives: 21.5 us -> none  [shards(): lax.all_to_all(grad_pooled_here.reshape(group_rows, 1, head_width).astype...]
    all_to_all x1 -> x0, starting transfers between devices: 18.8 us -> none  [side_by_side(): lax.all_to_all(both, axis, split_axis=split_dim, concat_axis=concat_dim,...]
    ppermute x4 -> x0, starting transfers between devices: 15.5 us -> none  [shifted_2(): lax.ppermute(value, axis, [(source, source + steps) for source in range(l...]
  transfers between devices with their start and end apart: 7 -> 0, of which waited for: 6 -> 0; matrix products, arithmetic and copies ran while one was open for 5% -> 0% of each run, Pallas kernels for 0% -> 0%
where the time goes in v1:
time: 104 us
  Pallas kernels  101 us (97%)
  local copies, waits for them, and re-layouts  2.51 us (2%)
    pallas_call x1, Pallas kernels, shards(): pl.pallas_call(functools.partial(kernel, sizes), out_shape=(jax.ShapeDtyp...  101 us
    unnamed x4, local copies, waits for them, and re-layouts  2.51 us

profile of v1, /device:TPU:1, one launch (start us, length us, event | category | flops | bytes accessed | tf_op | source)
XLA Modules:
  0.0 103.7 jit_solution(15919004071379272302)
XLA Ops:
  0.6 100.6 %hourglass.1 = (bf16[128,2048]{1,0:T(8,128)(2,1)}, f32[4,2048]{1,0:T(4,128)}) custom-call(bf16[128,2048]{1,0:T(8,128)(2,1)} %tok.1, bf16[128,2048]{1,0:T(8,128)(2,1)} %gout.1, f32[1,2048]{1,0:T(1,128)} %bitcast.4, f32[1,2048]{1,0:T(1,128)} %bitcast.5, f32[1,2048]{1,0:T(1,128)} %bitcast.6, f32[1,2048]{1,0:T(1,128)} %bitcast.7), custom_call_target="tpu_custom_call" | custom-call | tf_op jit(solution)/shard_map/hourglass/pallas_call | solution.py:513
  101.2 0.0 copy-start
  101.2 1.9 %copy.10 = bf16[128,2048]{1,0:T(8,128)(2,1)} copy(bf16[128,2048]{1,0:T(8,128)(2,1)} %get-tuple-element.4) | data formatting | bytes 1048576
  103.1 0.0 copy-done
  103.1 0.6 copy.11
Async XLA Ops:
  101.2 1.9 %copy-start = (f32[4,2048]{1,0:T(4,128)S(1)}, f32[4,2048]{1,0:T(4,128)}, u32[]{:S(2)}) copy-start(f32[4,2048]{1,0:T(4,128)} %get-tuple-element.5) | copy-start | bytes 98308

commit v2 on v1

v2 whole, which is shorter than its diff:
```python
import functools

import jax
import jax.numpy as jnp
from jax import lax
from jax.experimental import pallas as pl
from jax.experimental.pallas import tpu as pltpu
from jax.sharding import Mesh
from jax.sharding import PartitionSpec as P

AXES = ("zh", "y", "x", "zl", "c")
MESH = pl.DeviceIdType.MESH
T = 128
HD = 128
SLOTS = 8
NEGATIVE = -1e30
TEMPER = HD ** (-0.5)
F32 = jnp.float32
BF16 = jnp.bfloat16
GROUP = 4


def mm(a, b):
    return jnp.dot(a, b, preferred_element_type=F32)


def mm_nt(a, b):
    return lax.dot_general(a, b, (((1,), (1,)), ((), ())), preferred_element_type=F32)


def mm_tn(a, b):
    return lax.dot_general(a, b, (((0,), (0,)), ((), ())), preferred_element_type=F32)


def iota(shape, dim):
    return lax.broadcasted_iota(jnp.int32, shape, dim)


def remote(src, dst, send, recv, device):
    return pltpu.make_async_remote_copy(
        src_ref=src, dst_ref=dst, send_sem=send, recv_sem=recv, device_id=device, device_id_type=MESH
    )


def loop(count, body, start=0):
    def step(k, carry):
        body(k)
        return carry

    lax.fori_loop(start, count, step, 0)


def kernel(
    sizes,
    tok, gout, qg, kg, sqg, skg,
    out, gains,
    ctx, gsrc, tnext, qs, ks, own_scores, short, ext, wt, ws, pg_send, pg_recv, pgx, kz, prob, dprob, ds_short, stats,
    qgr_send, qgr_recv, kgr_send, kgr_recv, gp_send, gp_recv, gp_prev,
    gm, ds_local, gk_local, ret_send, ret_recv, acc, outv, gr_send, gr_recv, gx, gz, gfin,
    load_sem, next_send, next_recv, tok_send, tok_recv, a_send, a_recv, x_send, x_recv, z_send, z_recv,
    prev_send, prev_recv,
):
    nzh, ny, nx, nzl, nc = sizes
    nz, na = nzh * nzl, ny * nc
    heads = na
    span = na * SLOTS
    zh, y, x, zl, c = [lax.axis_index(name) for name in AXES]
    z = zh * nzl + zl
    a = y * nc + c
    chain = (((zh * ny + y) * nx + x) * nzl + zl) * nc + c
    total = nzh * ny * nx * nzl * nc

    def decode(index):
        return (
            index // (ny * nx * nzl * nc),
            index // (nx * nzl * nc) % ny,
            index // (nzl * nc) % nx,
            index // nc % nzl,
            index % nc,
        )

    following = decode((chain + 1) % total)
    previous = decode((chain + total - 1) % total)

    def at_a(other):
        return (zh, other // nc, x, zl, other % nc)

    def at_x(other):
        return (zh, y, other, zl, c)

    def at_z(other):
        return (other // nzl, y, x, other % nzl, c)

    barrier = pltpu.get_barrier_semaphore()
    drains = []

    def greet(device):
        pl.semaphore_signal(barrier, inc=1, device_id=device, device_id_type=MESH)

    greet(following)
    greet(previous)
    loop(na, lambda k: greet(at_a((a + k) % na)), 1)
    loop(nz, lambda k: greet(at_z((z + k) % nz)), 1)
    loop(nx, lambda k: greet(at_x((x + k) % nx)), 1)

    load_tok = pltpu.make_async_copy(tok, ctx.at[pl.ds(T, T)], load_sem.at[0])
    load_gout = pltpu.make_async_copy(gout, gsrc.at[pl.ds(0, T)], load_sem.at[1])
    load_tok.start()
    load_gout.start()

    pl.semaphore_wait(barrier, 2 + (na - 1) + (nz - 1) + (nx - 1))

    def columns(h):
        return pl.ds(pl.multiple_of(h * HD, HD), HD)

    head_tok = remote(tok.at[pl.ds(0, 16)], tnext, next_send.at[0], next_recv.at[0], previous)
    head_gout = remote(gout.at[pl.ds(0, 16)], gsrc.at[pl.ds(T, 16)], next_send.at[1], next_recv.at[1], previous)
    head_tok.start()
    head_gout.start()
    drains.append(head_tok.wait_send)
    drains.append(head_gout.wait_send)

    def tokens_of(h):
        return remote(
            tok.at[:, columns(h)], ctx.at[pl.ds(0, T), columns(h)], tok_send.at[h], tok_recv.at[h], following
        )

    loop(heads, lambda h: tokens_of(h).start())
    drains.append(lambda: loop(heads, lambda h: tokens_of(h).wait_send()))

    key_row = iota((T, T), 0)
    query_col = iota((T, T), 1)
    prior = key_row > query_col
    first_bias = jnp.where(chain == 0, NEGATIVE, 0.0)
    last_bias = jnp.where(chain == total - 1, NEGATIVE, 0.0)
    not_last = jnp.where(chain == total - 1, 0.0, 1.0)
    self_lane = iota((SLOTS, T), 1) == 0
    slot = iota((SLOTS, T), 0)
    row = iota((SLOTS, T), 1)
    keep = jnp.where(slot == SLOTS - 1, not_last, 1.0)
    pool = jnp.where((row > slot * 16) & (row <= slot * 16 + 16), keep, 0.0).astype(BF16)
    gpool = jnp.where((row >= slot * 16 + 16) & (row < slot * 16 + 32), 1.0, 0.0).astype(BF16)
    tail = iota((SLOTS, HD), 0) == SLOTS - 1

    load_tok.wait()
    load_gout.wait()

    def grouped(body):
        def several(g):
            for u in range(GROUP):
                body(g * GROUP + u)

        loop(heads // GROUP, several)

    def prepare(h):
        cols = columns(h)
        own_f = ctx[pl.ds(T, T), cols].astype(F32)
        queries = (own_f * qg[:, cols]).astype(BF16)
        keys = (own_f * kg[:, cols]).astype(BF16)
        qs[h] = queries
        ks[h] = keys
        own_scores[h] = mm_nt(keys, queries) * TEMPER
        short[h] = mm(gpool, gsrc[pl.ds(0, T), cols])

    grouped(prepare)
    head_tok.wait_recv()
    head_gout.wait_recv()

    def extend(h):
        cols = columns(h)
        ext_f = tnext[:, cols].astype(F32)[:SLOTS]
        queries = (ext_f * qg[:, cols]).astype(BF16)
        keys = (ext_f * kg[:, cols]).astype(BF16)
        same = (queries.astype(F32) * keys.astype(F32)).sum(axis=1, keepdims=True) * TEMPER
        scores = jnp.where(self_lane, same, mm_nt(queries, ks[h]) * TEMPER + last_bias)
        weights = jnp.exp(scores - scores.max(axis=1, keepdims=True))
        weights = (weights * (1.0 / weights.sum(axis=1, keepdims=True))).astype(BF16).astype(F32)
        found = mm(jnp.where(self_lane, 0.0, weights).astype(BF16), ctx[pl.ds(T, T), cols])
        found = found + weights[:, 0:1] * ext_f
        ext[h] = (ext_f + found).astype(BF16).astype(F32)
        next_sum = gsrc[pl.ds(T, 16), cols].astype(F32).sum(axis=0, keepdims=True)
        short[h] += jnp.where(tail, next_sum, 0.0)

    grouped(extend)

    def exchange(kind, h):
        send, recv, ssem, rsem = kind
        return remote(send.at[h], recv.at[a], ssem.at[h], rsem.at[a], at_a(h))

    def arrived(kind, h):
        send, recv, ssem, rsem = kind
        remote(send.at[h], recv.at[h], ssem.at[h], rsem.at[h], at_a(h)).wait_recv()

    def others_a(body):
        loop(na, lambda k: body((a + k) % na), 1)

    pg_kind = (pg_send, pg_recv, a_send.at[0], a_recv.at[0])
    gp_kind = (gp_send, gp_recv, a_send.at[1], a_recv.at[1])
    gr_kind = (gr_send, gr_recv, a_send.at[2], a_recv.at[2])

    def forward(h):
        cols = columns(h)
        both = ctx[:, cols]
        both_f = both.astype(F32)
        keys = (both_f[:T] * kg[:, cols]).astype(BF16)
        scores = jnp.where(prior, mm_nt(keys, qs[h]) * TEMPER + first_bias, own_scores[h])
        weights = jnp.exp(scores - scores.max(axis=0, keepdims=True))
        weights = weights * (1.0 / weights.sum(axis=0, keepdims=True))
        wt[h] = weights
        split = jnp.concatenate([jnp.where(prior, weights, 0.0), jnp.where(prior, 0.0, weights)], axis=0).astype(BF16)
        ws[h] = split
        mixed = (both_f[T:] + mm_tn(split, both)).astype(BF16)
        pooled = mm(pool, mixed) + jnp.where(tail, ext[h][0:1], 0.0)
        pg_send[h] = jnp.concatenate([pooled * (1.0 / 16), short[h]], axis=0).astype(BF16)

        @pl.when(h != a)
        def _():
            exchange(pg_kind, h).start()

        @pl.when(h == a)
        def _():
            pg_recv[h] = pg_send[h]

    def forward_group(g):
        for u in range(GROUP):
            tokens_of(g * GROUP + u).wait_recv()
        for u in range(GROUP):
            forward(g * GROUP + u)

    loop(heads // GROUP, forward_group)
    others_a(lambda h: arrived(pg_kind, h))
    drains.append(lambda: others_a(lambda h: exchange(pg_kind, h).wait_send()))

    blocks = pg_recv[...].astype(F32)
    pooled_own = blocks[:, :SLOTS].reshape(span, HD).astype(BF16)
    short_own = blocks[:, SLOTS:].reshape(span, HD)
    pgx[x, 0] = pooled_own
    pgx[x, 1] = short_own.astype(BF16)
    kz[z] = pooled_own

    def gather_x(other):
        return remote(pgx.at[x], pgx.at[x], x_send.at[0, other], x_recv.at[0, x], at_x(other))

    def gather_z(other):
        return remote(kz.at[z], kz.at[z], z_send.at[0, other], z_recv.at[0, z], at_z(other))

    def others_x(body):
        loop(nx, lambda k: body((x + k) % nx), 1)

    def others_z(body):
        loop(nz, lambda k: body((z + k) % nz), 1)

    def zig(k):
        half = (k + 1) // 2
        return (z + nz + half * (1 - 2 * ((k + 1) % 2))) % nz

    loop(nz - 1, lambda k: gather_z(zig(nz - 1 - k)).start())
    others_x(lambda o: gather_x(o).start())

    def x_arrived(phase, ref, other):
        remote(ref.at[other], ref.at[other], x_send.at[phase, other], x_recv.at[phase, other], at_x(other)).wait_recv()

    def z_arrived(phase, ref, other):
        remote(ref.at[other], ref.at[other], z_send.at[phase, other], z_recv.at[phase, other], at_z(other)).wait_recv()

    def position(zi, xi, index):
        source, place = index // SLOTS, index % SLOTS
        device = ((zi // nzl * ny + source // nc) * nx + xi) * nzl * nc + zi % nzl * nc + source % nc
        raw = device * SLOTS + place + 1
        return jnp.where(raw == total * SLOTS, 0, raw)

    head_cols = columns(a)
    gain_query = sqg[:, head_cols]
    gain_key = skg[:, head_cols]

    gain_both = gain_query * gain_key * TEMPER
    others_x(lambda o: x_arrived(0, pgx, o))
    wide = nx * span
    pooled_all = pgx[:, 0].reshape(wide, HD)
    short_all = pgx[:, 1].reshape(wide, HD)
    queries_all = (pooled_all.astype(F32) * gain_query).astype(BF16)
    query_index = iota((1, wide), 1)
    query_pos = position(z, query_index // span, query_index % span)
    key_index = iota((span, 1), 0)

    def first_pass(k, highest):
        b = zig(k)

        @pl.when(k > 0)
        def _():
            z_arrived(0, kz, b)

        values = kz[b]
        keys = (values.astype(F32) * gain_key).astype(BF16)
        visible = position(b, x, key_index) <= query_pos
        scores = jnp.where(visible, mm_nt(keys, queries_all) * TEMPER, NEGATIVE)
        prob[b] = scores
        dprob[b] = mm_nt(values, short_all)
        return jnp.maximum(highest, scores.max(axis=0, keepdims=True))

    highest = lax.fori_loop(0, nz, first_pass, jnp.full((1, wide), 0.1 * NEGATIVE, F32))
    drains.append(lambda: others_z(lambda o: gather_z(o).wait_send()))
    drains.append(lambda: others_x(lambda o: gather_x(o).wait_send()))

    def totals(b, carry):
        sums, dots = carry
        weights = jnp.exp(prob[b] - highest)
        prob[b] = weights
        return (
            sums + weights.sum(axis=0, keepdims=True),
            dots + (weights * dprob[b]).sum(axis=0, keepdims=True),
        )

    zero = jnp.zeros((1, wide), F32)
    sums, dots = lax.fori_loop(0, nz, totals, (zero, zero))
    stats[x] = jnp.concatenate([highest, sums, dots, jnp.zeros((5, wide), F32)], axis=0)

    def send_stats(other):
        return remote(stats.at[x], stats.at[x], x_send.at[1, other], x_recv.at[1, x], at_x(other))

    others_x(lambda o: send_stats(o).start())
    others_x(lambda o: x_arrived(1, stats, o))
    drains.append(lambda: others_x(lambda o: send_stats(o).wait_send()))

    def send_query(other):
        return remote(qgr_send.at[other], qgr_recv.at[x], x_send.at[2, other], x_recv.at[2, x], at_x(other))

    def send_key(other):
        return remote(kgr_send.at[other], kgr_recv.at[z], z_send.at[1, other], z_recv.at[1, z], at_z(other))

    pieces = [stats[s] for s in range(nx)]
    top = pieces[0][0:1]
    for piece in pieces[1:]:
        top = jnp.maximum(top, piece[0:1])
    all_sums = jnp.zeros((1, wide), F32)
    all_dots = jnp.zeros((1, wide), F32)
    for piece in pieces:
        factor = jnp.exp(piece[0:1] - top)
        all_sums = all_sums + piece[1:2] * factor
        all_dots = all_dots + piece[2:3] * factor
    inverse = 1.0 / all_sums
    mine = jnp.exp(highest - top) * inverse
    all_dots = all_dots * inverse

    def second_pass(k, gain_sum):
        b = zig(nz - 1 - k)
        weights = prob[b] * mine
        ds = (weights * (dprob[b] - all_dots)).astype(BF16)
        ds_short[b] = ds
        grad_k = mm(ds, pooled_all)
        grad_v = mm(weights.astype(BF16), short_all)
        kgr_send[b] = (grad_k * gain_both + grad_v).astype(BF16)

        @pl.when(k < nz - 1)
        def _():
            send_key(b).start()

        return gain_sum + (grad_k * kz[b].astype(F32)).sum(axis=0, keepdims=True)

    gain_short = lax.fori_loop(0, nz, second_pass, jnp.zeros((1, HD), F32))
    grad_q = mm_tn(ds_short[...].reshape(nz * span, wide), kz[...].reshape(nz * span, HD)) * gain_both
    qgr_send[...] = grad_q.astype(BF16).reshape(nx, span, HD)
    others_x(lambda o: send_query(o).start())
    qgr_recv[x] = qgr_send[x]
    kgr_recv[z] = kgr_send[z]
    drains.append(lambda: others_x(lambda o: send_query(o).wait_send()))
    drains.append(lambda: others_z(lambda o: send_key(o).wait_send()))
    others_x(lambda o: x_arrived(2, qgr_recv, o))
    others_z(lambda o: z_arrived(1, kgr_recv, o))
    grad_pooled = short_own + qgr_recv[...].astype(F32).sum(axis=0) + kgr_recv[...].astype(F32).sum(axis=0)
    gp_send[...] = grad_pooled.reshape(na, SLOTS, HD)
    others_a(lambda h: exchange(gp_kind, h).start())
    gp_recv[a] = gp_send[a]
    others_a(lambda h: arrived(gp_kind, h))
    drains.append(lambda: others_a(lambda h: exchange(gp_kind, h).wait_send()))
    pass_on = remote(gp_recv, gp_prev, next_send.at[2], next_recv.at[2], following)
    pass_on.start()
    pass_on.wait_recv()
    drains.append(pass_on.wait_send)

    token = iota((T, 16), 0)
    place = iota((T, 16), 1)
    source = jnp.where(token == 0, 15, (token + 15) // 16 - 1)
    spread = jnp.where(place == source, jnp.where(place == SLOTS - 1, not_last, 1.0) * (1.0 / 16), 0.0).astype(BF16)

    def give_back(h):
        return remote(ret_send.at[h], ret_recv.at[h], prev_send.at[h], prev_recv.at[h], previous)

    def scores_back(h):
        cols = columns(h)
        both = ctx[:, cols]
        rows = jnp.concatenate([gp_recv[h], gp_prev[h]], axis=0).astype(BF16)
        grad_mixed = gsrc[pl.ds(0, T), cols].astype(F32) + mm(spread, rows)
        acc[h] = grad_mixed
        incoming = grad_mixed.astype(BF16)
        gm[h] = incoming
        grads = mm_nt(both, incoming)
        grads = jnp.where(prior, grads[:T], grads[T:])
        weights = wt[h]
        dots = (weights * grads).sum(axis=0, keepdims=True)
        ds = weights * (grads - dots)
        ds = jnp.concatenate([jnp.where(prior, ds, 0.0), jnp.where(prior, 0.0, ds)], axis=0).astype(BF16)
        ds_local[h] = ds
        grad_k = mm(ds, both[T:])
        gk_local[h] = grad_k
        gain = (grad_k * both.astype(F32)).sum(axis=0, keepdims=True)
        gr_send[h] = jnp.concatenate([gain, jnp.zeros((7, HD), F32)], axis=0)

        @pl.when(h != a)
        def _():
            exchange(gr_kind, h).start()

        @pl.when(h == a)
        def _():
            gr_recv[h] = gr_send[h]

    grouped(scores_back)
    drains.append(lambda: others_a(lambda h: exchange(gr_kind, h).wait_send()))

    def values_back(h):
        cols = columns(h)
        gain = qg[:, cols] * kg[:, cols] * TEMPER
        to_keys = gk_local[h] * gain + mm(ws[h], gm[h])
        ret_send[h] = to_keys[:T].astype(BF16)
        give_back(h).start()
        acc[h] += mm_tn(ds_local[h], ctx[:, cols]) * gain + to_keys[T:]

    grouped(values_back)
    drains.append(lambda: loop(heads, lambda h: give_back(h).wait_send()))

    others_a(lambda h: arrived(gr_kind, h))
    short_rows = jnp.concatenate([jnp.zeros((1, HD), F32), gain_short, jnp.zeros((6, HD), F32)], axis=0)
    gx[x] = gr_recv[...].sum(axis=0) + short_rows

    def sum_x(other):
        return remote(gx.at[x], gx.at[x], x_send.at[3, other], x_recv.at[3, x], at_x(other))

    def sum_z(other):
        return remote(gz.at[z], gz.at[z], z_send.at[2, other], z_recv.at[2, z], at_z(other))

    def share(other):
        return remote(gfin.at[a], gfin.at[a], a_send.at[3, other], a_recv.at[3, a], at_a(other))

    others_x(lambda o: sum_x(o).start())
    others_x(lambda o: x_arrived(3, gx, o))
    drains.append(lambda: others_x(lambda o: sum_x(o).wait_send()))
    gz[z] = gx[...].sum(axis=0)
    others_z(lambda o: sum_z(o).start())
    others_z(lambda o: z_arrived(2, gz, o))
    drains.append(lambda: others_z(lambda o: sum_z(o).wait_send()))
    gfin[a] = gz[...].sum(axis=0) * (TEMPER * float(total * T) ** (-0.5))
    others_a(lambda h: share(h).start())
    drains.append(lambda: others_a(lambda h: share(h).wait_send()))

    def finish(h):
        give_back(h).wait_recv()
        outv[:, columns(h)] = (acc[h] + ret_recv[h].astype(F32)).astype(BF16)

    grouped(finish)
    store = pltpu.make_async_copy(outv, out, load_sem.at[2])
    store.start()
    drains.append(store.wait)
    others_a(
        lambda h: remote(gfin.at[h], gfin.at[h], a_send.at[3, h], a_recv.at[3, h], at_a(h)).wait_recv()
    )

    def put(h):
        cols = columns(h)
        local, pooled = gfin[h][0:1], gfin[h][1:2]
        rows = [local * kg[:, cols], local * qg[:, cols], pooled * skg[:, cols], pooled * sqg[:, cols]]
        gains[:, cols] = jnp.concatenate(rows, axis=0)

    grouped(put)
    for wait in drains:
        wait()


def shards(sizes, tokens, grad_output, query_gain, key_gain, short_query_gain, short_key_gain):
    nzh, ny, nx, nzl, nc = sizes
    nz, na = nzh * nzl, ny * nc
    width = tokens.shape[1]
    heads = width // HD
    span = na * SLOTS
    vmem = pl.BlockSpec(memory_space=pltpu.VMEM)
    hbm = pl.BlockSpec(memory_space=pl.ANY)
    dma = pltpu.SemaphoreType.DMA
    scratch = [
        pltpu.VMEM((2 * T, width), BF16),
        pltpu.VMEM((T + 16, width), BF16),
        pltpu.VMEM((16, width), BF16),
        pltpu.VMEM((heads, T, HD), BF16),
        pltpu.VMEM((heads, T, HD), BF16),
        pltpu.VMEM((heads, T, T), F32),
        pltpu.VMEM((heads, SLOTS, HD), F32),
        pltpu.VMEM((heads, SLOTS, HD), F32),
        pltpu.VMEM((heads, T, T), F32),
        pltpu.VMEM((heads, 2 * T, T), BF16),
        pltpu.VMEM((na, 16, HD), BF16),
        pltpu.VMEM((na, 16, HD), BF16),
        pltpu.VMEM((nx, 2, span, HD), BF16),
        pltpu.VMEM((nz, span, HD), BF16),
        pltpu.VMEM((nz, span, nx * span), F32),
        pltpu.VMEM((nz, span, nx * span), F32),
        pltpu.VMEM((nz, span, nx * span), BF16),
        pltpu.VMEM((nx, 8, nx * span), F32),
        pltpu.VMEM((nx, span, HD), BF16),
        pltpu.VMEM((nx, span, HD), BF16),
        pltpu.VMEM((nz, span, HD), BF16),
        pltpu.VMEM((nz, span, HD), BF16),
        pltpu.VMEM((na, SLOTS, HD), F32),
        pltpu.VMEM((na, SLOTS, HD), F32),
        pltpu.VMEM((na, SLOTS, HD), F32),
        pltpu.VMEM((heads, T, HD), BF16),
        pltpu.VMEM((heads, 2 * T, T), BF16),
        pltpu.VMEM((heads, 2 * T, HD), F32),
        pltpu.VMEM((heads, T, HD), BF16),
        pltpu.VMEM((heads, T, HD), BF16),
        pltpu.VMEM((heads, T, HD), F32),
        pltpu.VMEM((T, width), BF16),
        pltpu.VMEM((na, 8, HD), F32),
        pltpu.VMEM((na, 8, HD), F32),
        pltpu.VMEM((nx, 8, HD), F32),
        pltpu.VMEM((nz, 8, HD), F32),
        pltpu.VMEM((na, 8, HD), F32),
        dma((3,)),
        dma((3,)),
        dma((3,)),
        dma((heads,)),
        dma((heads,)),
        dma((4, na)),
        dma((4, na)),
        dma((4, nx)),
        dma((4, nx)),
        dma((3, nz)),
        dma((3, nz)),
        dma((heads,)),
        dma((heads,)),
    ]
    return pl.pallas_call(
        functools.partial(kernel, sizes),
        out_shape=(
            jax.ShapeDtypeStruct(tokens.shape, BF16),
            jax.ShapeDtypeStruct((4, width), F32),
        ),
        in_specs=[hbm, hbm, vmem, vmem, vmem, vmem],
        out_specs=(hbm, vmem),
        scratch_shapes=scratch,
        compiler_params=pltpu.CompilerParams(collective_id=0, has_side_effects=True),
        name="hourglass",
    )(
        tokens,
        grad_output,
        query_gain.reshape(1, width),
        key_gain.reshape(1, width),
        short_query_gain.reshape(1, width),
        short_key_gain.reshape(1, width),
    )


def build(mesh, sizes):
    finer = Mesh(mesh.devices.reshape(sizes), AXES)
    return jax.shard_map(
        functools.partial(shards, sizes),
        mesh=finer,
        in_specs=(P(AXES, None), P(AXES, None), P(), P(), P(), P()),
        out_specs=(P(AXES, None), P()),
        check_vma=False,
    )


def solution(mesh):
    return build(mesh, (2, 8, 4, 4, 2))
```

time: 104 us -> 104 us (level)
  no operation moved by 1% of the time
where the time goes in v2:
time: 104 us
  Pallas kernels  101 us (97%)
  local copies, waits for them, and re-layouts  2.51 us (2%)
    pallas_call x1, Pallas kernels, shards(): pl.pallas_call(functools.partial(kernel, sizes), out_shape=(jax.ShapeDtyp...  101 us
    unnamed x4, local copies, waits for them, and re-layouts  2.51 us

profile of v2, /device:TPU:1, one launch (start us, length us, event | category | flops | bytes accessed | tf_op | source)
XLA Modules:
  0.0 104.2 jit_solution(11300790429407718100)
XLA Ops:
  0.6 101.0 %hourglass.1 = (bf16[128,2048]{1,0:T(8,128)(2,1)}, f32[4,2048]{1,0:T(4,128)}) custom-call(bf16[128,2048]{1,0:T(8,128)(2,1)} %tok.1, bf16[128,2048]{1,0:T(8,128)(2,1)} %gout.1, f32[1,2048]{1,0:T(1,128)} %bitcast.4, f32[1,2048]{1,0:T(1,128)} %bitcast.5, f32[1,2048]{1,0:T(1,128)} %bitcast.6, f32[1,2048]{1,0:T(1,128)} %bitcast.7), custom_call_target="tpu_custom_call" | custom-call | tf_op jit(solution)/shard_map/hourglass/pallas_call | solution.py:539
  101.7 0.0 copy-start
  101.7 1.9 %copy.10 = bf16[128,2048]{1,0:T(8,128)(2,1)} copy(bf16[128,2048]{1,0:T(8,128)(2,1)} %get-tuple-element.4) | data formatting | bytes 1048576
  103.6 0.0 copy-done
  103.6 0.6 copy.11
Async XLA Ops:
  101.7 1.9 %copy-start = (f32[4,2048]{1,0:T(4,128)S(1)}, f32[4,2048]{1,0:T(4,128)}, u32[]{:S(2)}) copy-start(f32[4,2048]{1,0:T(4,128)} %get-tuple-element.5) | copy-start | bytes 98308

commit v3 on v2

--- a/solution.py
+++ b/solution.py
@@ -17,7 +17,7 @@
 TEMPER = HD ** (-0.5)
 F32 = jnp.float32
 BF16 = jnp.bfloat16
-GROUP = 4
+GROUP = 8
 
 
 def mm(a, b):
@@ -63,6 +63,7 @@
     nzh, ny, nx, nzl, nc = sizes
     nz, na = nzh * nzl, ny * nc
     heads = na
+    group = min(GROUP, heads)
     span = na * SLOTS
     zh, y, x, zl, c = [lax.axis_index(name) for name in AXES]
     z = zh * nzl + zl
@@ -145,12 +146,15 @@
     load_tok.wait()
     load_gout.wait()
 
-    def grouped(body):
+    def grouped(body, kind=None):
         def several(g):
-            for u in range(GROUP):
-                body(g * GROUP + u)
-
-        loop(heads // GROUP, several)
+            for u in range(group):
+                body(g * group + u)
+            if kind is not None:
+                for u in range(group):
+                    dispatch(kind, g * group + u)
+
+        loop(heads // group, several)
 
     def prepare(h):
         cols = columns(h)
@@ -171,17 +175,26 @@
         ext_f = tnext[:, cols].astype(F32)[:SLOTS]
         queries = (ext_f * qg[:, cols]).astype(BF16)
         keys = (ext_f * kg[:, cols]).astype(BF16)
-        same = (queries.astype(F32) * keys.astype(F32)).sum(axis=1, keepdims=True) * TEMPER
-        scores = jnp.where(self_lane, same, mm_nt(queries, ks[h]) * TEMPER + last_bias)
-        weights = jnp.exp(scores - scores.max(axis=1, keepdims=True))
-        weights = (weights * (1.0 / weights.sum(axis=1, keepdims=True))).astype(BF16).astype(F32)
+        products = queries.astype(F32) * keys.astype(F32)
+        same = jnp.broadcast_to(products.sum(axis=1, keepdims=True), (SLOTS, T))
+        ext[h] = jnp.where(self_lane, same, mm_nt(queries, ks[h]) + last_bias) * TEMPER
+        next_sum = gsrc[pl.ds(T, 16), cols].astype(F32).sum(axis=0, keepdims=True)
+        short[h] += jnp.where(tail, next_sum, 0.0)
+
+    def extend_values(h):
+        cols = columns(h)
+        ext_f = tnext[:, cols].astype(F32)[:SLOTS]
+        weights = ext[h]
         found = mm(jnp.where(self_lane, 0.0, weights).astype(BF16), ctx[pl.ds(T, T), cols])
         found = found + weights[:, 0:1] * ext_f
         ext[h] = (ext_f + found).astype(BF16).astype(F32)
-        next_sum = gsrc[pl.ds(T, 16), cols].astype(F32).sum(axis=0, keepdims=True)
-        short[h] += jnp.where(tail, next_sum, 0.0)
 
     grouped(extend)
+    ext_weights = ext[...]
+    ext_weights = jnp.exp(ext_weights - ext_weights.max(axis=2, keepdims=True))
+    ext_weights = ext_weights * (1.0 / ext_weights.sum(axis=2, keepdims=True))
+    ext[...] = ext_weights.astype(BF16).astype(F32)
+    grouped(extend_values)
 
     def exchange(kind, h):
         send, recv, ssem, rsem = kind
@@ -213,21 +226,21 @@
         pooled = mm(pool, mixed) + jnp.where(tail, ext[h][0:1], 0.0)
         pg_send[h] = jnp.concatenate([pooled * (1.0 / 16), short[h]], axis=0).astype(BF16)
 
+    def dispatch(kind, h):
         @pl.when(h != a)
         def _():
-            exchange(pg_kind, h).start()
-
-        @pl.when(h == a)
-        def _():
-            pg_recv[h] = pg_send[h]
+            exchange(kind, h).start()
 
     def forward_group(g):
-        for u in range(GROUP):
-            tokens_of(g * GROUP + u).wait_recv()
-        for u in range(GROUP):
-            forward(g * GROUP + u)
-
-    loop(heads // GROUP, forward_group)
+        for u in range(group):
+            tokens_of(g * group + u).wait_recv()
+        for u in range(group):
+            forward(g * group + u)
+        for u in range(group):
+            dispatch(pg_kind, g * group + u)
+
+    loop(heads // group, forward_group)
+    pg_recv[a] = pg_send[a]
     others_a(lambda h: arrived(pg_kind, h))
     drains.append(lambda: others_a(lambda h: exchange(pg_kind, h).wait_send()))
 
@@ -406,15 +419,8 @@
         gain = (grad_k * both.astype(F32)).sum(axis=0, keepdims=True)
         gr_send[h] = jnp.concatenate([gain, jnp.zeros((7, HD), F32)], axis=0)
 
-        @pl.when(h != a)
-        def _():
-            exchange(gr_kind, h).start()
-
-        @pl.when(h == a)
-        def _():
-            gr_recv[h] = gr_send[h]
-
-    grouped(scores_back)
+    grouped(scores_back, gr_kind)
+    gr_recv[a] = gr_send[a]
     drains.append(lambda: others_a(lambda h: exchange(gr_kind, h).wait_send()))
 
     def values_back(h):
@@ -422,10 +428,15 @@
         gain = qg[:, cols] * kg[:, cols] * TEMPER
         to_keys = gk_local[h] * gain + mm(ws[h], gm[h])
         ret_send[h] = to_keys[:T].astype(BF16)
-        give_back(h).start()
         acc[h] += mm_tn(ds_local[h], ctx[:, cols]) * gain + to_keys[T:]
 
-    grouped(values_back)
+    def values_group(g):
+        for u in range(group):
+            values_back(g * group + u)
+        for u in range(group):
+            give_back(g * group + u).start()
+
+    loop(heads // group, values_group)
     drains.append(lambda: loop(heads, lambda h: give_back(h).wait_send()))
 
     others_a(lambda h: arrived(gr_kind, h))

time: 104 us -> 93.6 us (0.90)
  Pallas kernels: 101 us -> 90.3 us
    pallas_call x1, Pallas kernels: 101 us -> 90.3 us  [shards(): pl.pallas_call(functools.partial(kernel, sizes), out_shape=(jax.ShapeDtyp...]
where the time goes in v3:
time: 93.6 us; the launch traced here: 93.4 us
  Pallas kernels  90.3 us (96%)
  local copies, waits for them, and re-layouts  2.51 us (3%)
    pallas_call x1, Pallas kernels, shards(): pl.pallas_call(functools.partial(kernel, sizes), out_shape=(jax.ShapeDtyp...  90.3 us
    unnamed x4, local copies, waits for them, and re-layouts  2.51 us

profile of v3, /device:TPU:1, one launch (start us, length us, event | category | flops | bytes accessed | tf_op | source)
XLA Modules:
  0.0 93.4 jit_solution(7631753856765987344)
XLA Ops:
  0.6 90.3 %hourglass.1 = (bf16[128,2048]{1,0:T(8,128)(2,1)}, f32[4,2048]{1,0:T(4,128)}) custom-call(bf16[128,2048]{1,0:T(8,128)(2,1)} %tok.1, bf16[128,2048]{1,0:T(8,128)(2,1)} %gout.1, f32[1,2048]{1,0:T(1,128)} %bitcast.4, f32[1,2048]{1,0:T(1,128)} %bitcast.5, f32[1,2048]{1,0:T(1,128)} %bitcast.6, f32[1,2048]{1,0:T(1,128)} %bitcast.7), custom_call_target="tpu_custom_call" | custom-call | tf_op jit(solution)/shard_map/hourglass/pallas_call | solution.py:550
  90.9 0.0 copy-start
  90.9 1.9 %copy.10 = bf16[128,2048]{1,0:T(8,128)(2,1)} copy(bf16[128,2048]{1,0:T(8,128)(2,1)} %get-tuple-element.4) | data formatting | bytes 1048576
  92.8 0.0 copy-done
  92.8 0.6 copy.11
Async XLA Ops:
  90.9 1.9 %copy-start = (f32[4,2048]{1,0:T(4,128)S(1)}, f32[4,2048]{1,0:T(4,128)}, u32[]{:S(2)}) copy-start(f32[4,2048]{1,0:T(4,128)} %get-tuple-element.5) | copy-start | bytes 98308

commit v4 on v3

--- a/solution.py
+++ b/solution.py
@@ -56,14 +56,16 @@
     out, gains,
     ctx, gsrc, tnext, qs, ks, own_scores, short, ext, wt, ws, pg_send, pg_recv, pgx, kz, prob, dprob, ds_short, stats,
     qgr_send, qgr_recv, kgr_send, kgr_recv, gp_send, gp_recv, gp_prev,
-    gm, ds_local, gk_local, ret_send, ret_recv, acc, outv, gr_send, gr_recv, gx, gz, gfin,
+    gm, ds_local, gk_local, ret_send, ret_recv, acc, outv, gsum, gpart, gx, gy, gz, gfin,
     load_sem, next_send, next_recv, tok_send, tok_recv, a_send, a_recv, x_send, x_recv, z_send, z_recv,
-    prev_send, prev_recv,
+    prev_send, prev_recv, c_send, c_recv, y_send, y_recv,
 ):
     nzh, ny, nx, nzl, nc = sizes
     nz, na = nzh * nzl, ny * nc
     heads = na
     group = min(GROUP, heads)
+    half = heads // 2
+    stride = min(4, heads)
     span = na * SLOTS
     zh, y, x, zl, c = [lax.axis_index(name) for name in AXES]
     z = zh * nzl + zl
@@ -146,13 +148,10 @@
     load_tok.wait()
     load_gout.wait()
 
-    def grouped(body, kind=None):
+    def grouped(body):
         def several(g):
             for u in range(group):
                 body(g * group + u)
-            if kind is not None:
-                for u in range(group):
-                    dispatch(kind, g * group + u)
 
         loop(heads // group, several)
 
@@ -209,7 +208,6 @@
 
     pg_kind = (pg_send, pg_recv, a_send.at[0], a_recv.at[0])
     gp_kind = (gp_send, gp_recv, a_send.at[1], a_recv.at[1])
-    gr_kind = (gr_send, gr_recv, a_send.at[2], a_recv.at[2])
 
     def forward(h):
         cols = columns(h)
@@ -232,14 +230,14 @@
             exchange(kind, h).start()
 
     def forward_group(g):
-        for u in range(group):
-            tokens_of(g * group + u).wait_recv()
-        for u in range(group):
-            forward(g * group + u)
-        for u in range(group):
-            dispatch(pg_kind, g * group + u)
-
-    loop(heads // group, forward_group)
+        for u in range(stride):
+            tokens_of(g * stride + u).wait_recv()
+        for u in range(stride):
+            forward(g * stride + u)
+        for u in range(stride):
+            dispatch(pg_kind, g * stride + u)
+
+    loop(heads // stride, forward_group)
     pg_recv[a] = pg_send[a]
     others_a(lambda h: arrived(pg_kind, h))
     drains.append(lambda: others_a(lambda h: exchange(pg_kind, h).wait_send()))
@@ -315,18 +313,18 @@
     drains.append(lambda: others_z(lambda o: gather_z(o).wait_send()))
     drains.append(lambda: others_x(lambda o: gather_x(o).wait_send()))
 
-    def totals(b, carry):
+    def totals(k, carry):
         sums, dots = carry
-        weights = jnp.exp(prob[b] - highest)
-        prob[b] = weights
-        return (
-            sums + weights.sum(axis=0, keepdims=True),
-            dots + (weights * dprob[b]).sum(axis=0, keepdims=True),
-        )
+        for b in (2 * k, 2 * k + 1):
+            weights = jnp.exp(prob[b] - highest)
+            prob[b] = weights
+            sums = sums + weights.sum(axis=0, keepdims=True)
+            dots = dots + (weights * dprob[b]).sum(axis=0, keepdims=True)
+        return sums, dots
 
     zero = jnp.zeros((1, wide), F32)
-    sums, dots = lax.fori_loop(0, nz, totals, (zero, zero))
-    stats[x] = jnp.concatenate([highest, sums, dots, jnp.zeros((5, wide), F32)], axis=0)
+    sums, dots = lax.fori_loop(0, nz // 2, totals, (zero, zero))
+    stats[x] = jnp.concatenate([highest, sums, dots, jnp.zeros((1, wide), F32)], axis=0)
 
     def send_stats(other):
         return remote(stats.at[x], stats.at[x], x_send.at[1, other], x_recv.at[1, x], at_x(other))
@@ -356,21 +354,26 @@
     all_dots = all_dots * inverse
 
     def second_pass(k, gain_sum):
-        b = zig(nz - 1 - k)
-        weights = prob[b] * mine
-        ds = (weights * (dprob[b] - all_dots)).astype(BF16)
-        ds_short[b] = ds
-        grad_k = mm(ds, pooled_all)
-        grad_v = mm(weights.astype(BF16), short_all)
-        kgr_send[b] = (grad_k * gain_both + grad_v).astype(BF16)
-
-        @pl.when(k < nz - 1)
+        for u in range(2):
+            b = zig(nz - 1 - 2 * k - u)
+            weights = prob[b] * mine
+            ds = (weights * (dprob[b] - all_dots)).astype(BF16)
+            ds_short[b] = ds
+            grad_k = mm(ds, pooled_all)
+            grad_v = mm(weights.astype(BF16), short_all)
+            kgr_send[b] = (grad_k * gain_both + grad_v).astype(BF16)
+            gain_sum = gain_sum + (grad_k * kz[b].astype(F32)).sum(axis=0, keepdims=True)
+        send_key(zig(nz - 1 - 2 * k)).start()
+
+        @pl.when(2 * k + 1 < nz - 1)
         def _():
-            send_key(b).start()
-
-        return gain_sum + (grad_k * kz[b].astype(F32)).sum(axis=0, keepdims=True)
-
-    gain_short = lax.fori_loop(0, nz, second_pass, jnp.zeros((1, HD), F32))
+            send_key(zig(nz - 2 - 2 * k)).start()
+
+        return gain_sum
+
+    gain_short = lax.fori_loop(0, nz // 2, second_pass, jnp.zeros((1, HD), F32))
+    gsum[...] = jnp.zeros_like(gsum)
+    gsum[a // half, pl.ds(half + a % half, 1), :] = gain_short
     grad_q = mm_tn(ds_short[...].reshape(nz * span, wide), kz[...].reshape(nz * span, HD)) * gain_both
     qgr_send[...] = grad_q.astype(BF16).reshape(nx, span, HD)
     others_x(lambda o: send_query(o).start())
@@ -417,11 +420,28 @@
         grad_k = mm(ds, both[T:])
         gk_local[h] = grad_k
         gain = (grad_k * both.astype(F32)).sum(axis=0, keepdims=True)
-        gr_send[h] = jnp.concatenate([gain, jnp.zeros((7, HD), F32)], axis=0)
-
-    grouped(scores_back, gr_kind)
-    gr_recv[a] = gr_send[a]
-    drains.append(lambda: others_a(lambda h: exchange(gr_kind, h).wait_send()))
+        gsum[h // half, pl.ds(h % half, 1), :] = gain
+
+    partner = (zh, y, x, zl, 1 - c)
+
+    def at_y(other):
+        return (zh, other, x, zl, c)
+
+    def others_y(body):
+        loop(ny, lambda k: body((y + k) % ny), 1)
+
+    halve = remote(gsum.at[1 - c], gpart, c_send.at[0], c_recv.at[0], partner)
+    share = remote(gfin.at[c], gfin.at[c], c_send.at[1], c_recv.at[1], partner)
+
+    def sum_z(other):
+        return remote(gz.at[z], gz.at[z], z_send.at[2, other], z_recv.at[2, z], at_z(other))
+
+    def sum_x(other):
+        return remote(gx.at[x], gx.at[x], x_send.at[3, other], x_recv.at[3, x], at_x(other))
+
+    def sum_y(other):
+        return remote(gy.at[y], gy.at[y], y_send.at[other], y_recv.at[y], at_y(other))
+
 
     def values_back(h):
         cols = columns(h)
@@ -436,32 +456,29 @@
         for u in range(group):
             give_back(g * group + u).start()
 
-    loop(heads // group, values_group)
+    grouped(scores_back)
+    halve.start()
+    values_group(0)
+    halve.wait_recv()
+    gy[y] = (gsum[c] + gpart[...]).astype(BF16)
+    others_y(lambda o: sum_y(o).start())
+    loop(heads // group, values_group, 1)
+    drains.append(halve.wait_send)
     drains.append(lambda: loop(heads, lambda h: give_back(h).wait_send()))
-
-    others_a(lambda h: arrived(gr_kind, h))
-    short_rows = jnp.concatenate([jnp.zeros((1, HD), F32), gain_short, jnp.zeros((6, HD), F32)], axis=0)
-    gx[x] = gr_recv[...].sum(axis=0) + short_rows
-
-    def sum_x(other):
-        return remote(gx.at[x], gx.at[x], x_send.at[3, other], x_recv.at[3, x], at_x(other))
-
-    def sum_z(other):
-        return remote(gz.at[z], gz.at[z], z_send.at[2, other], z_recv.at[2, z], at_z(other))
-
-    def share(other):
-        return remote(gfin.at[a], gfin.at[a], a_send.at[3, other], a_recv.at[3, a], at_a(other))
-
+    drains.append(lambda: others_y(lambda o: sum_y(o).wait_send()))
+
+    others_y(lambda o: remote(gy.at[o], gy.at[o], y_send.at[o], y_recv.at[o], at_y(o)).wait_recv())
+    gx[x] = gy[...].astype(F32).sum(axis=0).astype(BF16)
     others_x(lambda o: sum_x(o).start())
     others_x(lambda o: x_arrived(3, gx, o))
     drains.append(lambda: others_x(lambda o: sum_x(o).wait_send()))
-    gz[z] = gx[...].sum(axis=0)
+    gz[z] = gx[...].astype(F32).sum(axis=0).astype(BF16)
     others_z(lambda o: sum_z(o).start())
     others_z(lambda o: z_arrived(2, gz, o))
     drains.append(lambda: others_z(lambda o: sum_z(o).wait_send()))
-    gfin[a] = gz[...].sum(axis=0) * (TEMPER * float(total * T) ** (-0.5))
-    others_a(lambda h: share(h).start())
-    drains.append(lambda: others_a(lambda h: share(h).wait_send()))
+    gfin[c] = gz[...].astype(F32).sum(axis=0) * (TEMPER * float(total * T) ** (-0.5))
+    share.start()
+    drains.append(share.wait_send)
 
     def finish(h):
         give_back(h).wait_recv()
@@ -471,19 +488,33 @@
     store = pltpu.make_async_copy(outv, out, load_sem.at[2])
     store.start()
     drains.append(store.wait)
-    others_a(
-        lambda h: remote(gfin.at[h], gfin.at[h], a_send.at[3, h], a_recv.at[3, h], at_a(h)).wait_recv()
-    )
-
-    def put(h):
-        cols = columns(h)
-        local, pooled = gfin[h][0:1], gfin[h][1:2]
-        rows = [local * kg[:, cols], local * qg[:, cols], pooled * skg[:, cols], pooled * sqg[:, cols]]
-        gains[:, cols] = jnp.concatenate(rows, axis=0)
-
-    grouped(put)
+    remote(gfin.at[1 - c], gfin.at[1 - c], c_send.at[1], c_recv.at[1], partner).wait_recv()
+    for side in range(2):
+        rows = gfin[side]
+        for r in range(half):
+            cols = pl.ds((side * half + r) * HD, HD)
+            local, pooled = rows[r : r + 1], rows[half + r : half + r + 1]
+            gains[:, cols] = jnp.concatenate(
+                [local * kg[:, cols], local * qg[:, cols], pooled * skg[:, cols], pooled * sqg[:, cols]], axis=0
+            )
+
     for wait in drains:
         wait()
+
+
+def relay(first, second, out, gains, hold, small, arrive, leave):
+    rows = hold.shape[0] // 4
+    pairs = [(first.at[pl.ds(k * rows, rows)], hold.at[pl.ds(k * rows, rows)], out.at[pl.ds(k * rows, rows)]) for k in range(4)]
+    pairs.append((second, small, gains))
+    fetch = [pltpu.make_async_copy(i, m, arrive.at[k]) for k, (i, m, o) in enumerate(pairs)]
+    store = [pltpu.make_async_copy(m, o, leave.at[k]) for k, (i, m, o) in enumerate(pairs)]
+    for copy in fetch:
+        copy.start()
+    for k in range(5):
+        fetch[k].wait()
+        store[k].start()
+    for copy in store:
+        copy.wait()
 
 
 def shards(sizes, tokens, grad_output, query_gain, key_gain, short_query_gain, short_key_gain):
@@ -513,7 +544,7 @@
         pltpu.VMEM((nz, span, nx * span), F32),
         pltpu.VMEM((nz, span, nx * span), F32),
         pltpu.VMEM((nz, span, nx * span), BF16),
-        pltpu.VMEM((nx, 8, nx * span), F32),
+        pltpu.VMEM((nx, 4, nx * span), F32),
         pltpu.VMEM((nx, span, HD), BF16),
         pltpu.VMEM((nx, span, HD), BF16),
         pltpu.VMEM((nz, span, HD), BF16),
@@ -528,26 +559,31 @@
         pltpu.VMEM((heads, T, HD), BF16),
         pltpu.VMEM((heads, T, HD), F32),
         pltpu.VMEM((T, width), BF16),
-        pltpu.VMEM((na, 8, HD), F32),
-        pltpu.VMEM((na, 8, HD), F32),
-        pltpu.VMEM((nx, 8, HD), F32),
-        pltpu.VMEM((nz, 8, HD), F32),
-        pltpu.VMEM((na, 8, HD), F32),
+        pltpu.VMEM((2, heads, HD), F32),
+        pltpu.VMEM((heads, HD), F32),
+        pltpu.VMEM((nx, heads, HD), BF16),
+        pltpu.VMEM((ny, heads, HD), BF16),
+        pltpu.VMEM((nz, heads, HD), BF16),
+        pltpu.VMEM((2, heads, HD), F32),
         dma((3,)),
         dma((3,)),
         dma((3,)),
         dma((heads,)),
         dma((heads,)),
-        dma((4, na)),
-        dma((4, na)),
+        dma((2, na)),
+        dma((2, na)),
         dma((4, nx)),
         dma((4, nx)),
         dma((3, nz)),
         dma((3, nz)),
         dma((heads,)),
         dma((heads,)),
+        dma((2,)),
+        dma((2,)),
+        dma((ny,)),
+        dma((ny,)),
     ]
-    return pl.pallas_call(
+    first = pl.pallas_call(
         functools.partial(kernel, sizes),
         out_shape=(
             jax.ShapeDtypeStruct(tokens.shape, BF16),
@@ -566,6 +602,17 @@
         short_query_gain.reshape(1, width),
         short_key_gain.reshape(1, width),
     )
+    return pl.pallas_call(
+        relay,
+        out_shape=(
+            jax.ShapeDtypeStruct(tokens.shape, BF16),
+            jax.ShapeDtypeStruct((4, width), F32),
+        ),
+        in_specs=[hbm, hbm],
+        out_specs=(hbm, hbm),
+        scratch_shapes=[pltpu.VMEM(tokens.shape, BF16), pltpu.VMEM((4, width), F32), dma((5,)), dma((5,))],
+        name="relay",
+    )(*first)
 
 
 def build(mesh, sizes):

time: 93.6 us -> 89.6 us (0.957)
  local copies, waits for them, and re-layouts: 2.51 us -> 0 us
  Pallas kernels: 90.3 us -> 88 us
    pallas_call x1, Pallas kernels: 90.3 us -> 86.2 us  [shards(): pl.pallas_call(functools.partial(kernel, sizes), out_shape=(jax.ShapeDtyp...]
    unnamed x4 -> x0, local copies, waits for them, and re-layouts: 2.51 us -> none
    pallas_call x0 -> x1, Pallas kernels: none -> 1.84 us  [shards(): pl.pallas_call(relay, out_shape=(jax.ShapeDtypeStruct(tokens.shape, BF16)...]
where the time goes in v4:
time: 89.6 us; the launch traced here: 88.7 us
  Pallas kernels  88 us (98%)
    pallas_call x1, Pallas kernels, shards(): pl.pallas_call(functools.partial(kernel, sizes), out_shape=(jax.ShapeDtyp...  86.2 us
    pallas_call x1, Pallas kernels, shards(): pl.pallas_call(relay, out_shape=(jax.ShapeDtypeStruct(tokens.shape, BF16)...  1.84 us

profile of v4, /device:TPU:1, one launch (start us, length us, event | category | flops | bytes accessed | tf_op | source)
XLA Modules:
  0.0 88.7 jit_solution(6171913145494171635)
XLA Ops:
  0.6 86.2 %hourglass.1 = (bf16[128,2048]{1,0:T(8,128)(2,1)}, f32[4,2048]{1,0:T(4,128)}) custom-call(bf16[128,2048]{1,0:T(8,128)(2,1)} %tok.1, bf16[128,2048]{1,0:T(8,128)(2,1)} %gout.1, f32[1,2048]{1,0:T(1,128)} %bitcast.4, f32[1,2048]{1,0:T(1,128)} %bitcast.5, f32[1,2048]{1,0:T(1,128)} %bitcast.6, f32[1,2048]{1,0:T(1,128)} %bitcast.7), custom_call_target="tpu_custom_call" | custom-call | tf_op jit(solution)/shard_map/hourglass/pallas_call | solution.py:586
  86.8 1.8 %relay.1 = (bf16[128,2048]{1,0:T(8,128)(2,1)}, f32[4,2048]{1,0:T(4,128)}) custom-call(bf16[128,2048]{1,0:T(8,128)(2,1)} %get-tuple-element.4.first, f32[4,2048]{1,0:T(4,128)} %get-tuple-element.5.second), custom_call_target="tpu_custom_call" | custom-call | tf_op jit(solution)/shard_map/relay/pallas_call | solution.py:605

commit v5 on v4

--- a/solution.py
+++ b/solution.py
@@ -58,7 +58,7 @@
     qgr_send, qgr_recv, kgr_send, kgr_recv, gp_send, gp_recv, gp_prev,
     gm, ds_local, gk_local, ret_send, ret_recv, acc, outv, gsum, gpart, gx, gy, gz, gfin,
     load_sem, next_send, next_recv, tok_send, tok_recv, a_send, a_recv, x_send, x_recv, z_send, z_recv,
-    prev_send, prev_recv, c_send, c_recv, y_send, y_recv,
+    prev_send, prev_recv, d_send, d_recv, c_send, c_recv, y_send, y_recv,
 ):
     nzh, ny, nx, nzl, nc = sizes
     nz, na = nzh * nzl, ny * nc
@@ -385,14 +385,41 @@
     others_z(lambda o: z_arrived(1, kgr_recv, o))
     grad_pooled = short_own + qgr_recv[...].astype(F32).sum(axis=0) + kgr_recv[...].astype(F32).sum(axis=0)
     gp_send[...] = grad_pooled.reshape(na, SLOTS, HD)
+
+    def beyond(h):
+        after = (((zh * ny + h // nc) * nx + x) * nzl + zl) * nc + h % nc + 1
+        return remote(gp_send.at[h], gp_prev.at[a], d_send.at[h], d_recv.at[a], decode(after % total))
+
+    mine_next = jnp.where(c == 1, a - 1, heads)
+    mine_own = jnp.where(c == 1, a, heads)
+
+    def send_beyond(h):
+        @pl.when(h != mine_next)
+        def _():
+            beyond(h).start()
+
+    def drain_beyond(h):
+        @pl.when(h != mine_next)
+        def _():
+            beyond(h).wait_send()
+
+    def take_beyond(h):
+        @pl.when(h != mine_own)
+        def _():
+            remote(gp_send.at[h], gp_prev.at[h], d_send.at[h], d_recv.at[h], previous).wait_recv()
+
+    loop(heads, send_beyond)
     others_a(lambda h: exchange(gp_kind, h).start())
     gp_recv[a] = gp_send[a]
+
+    @pl.when(c == 1)
+    def _():
+        gp_prev[a] = gp_send[jnp.maximum(a - 1, 0)]
+
     others_a(lambda h: arrived(gp_kind, h))
+    loop(heads, take_beyond)
     drains.append(lambda: others_a(lambda h: exchange(gp_kind, h).wait_send()))
-    pass_on = remote(gp_recv, gp_prev, next_send.at[2], next_recv.at[2], following)
-    pass_on.start()
-    pass_on.wait_recv()
-    drains.append(pass_on.wait_send)
+    drains.append(lambda: loop(heads, drain_beyond))
 
     token = iota((T, 16), 0)
     place = iota((T, 16), 1)
@@ -578,6 +605,8 @@
         dma((3, nz)),
         dma((heads,)),
         dma((heads,)),
+        dma((heads,)),
+        dma((heads,)),
         dma((2,)),
         dma((2,)),
         dma((ny,)),

time: 89.6 us -> 87.2 us (0.973)
  Pallas kernels: 88 us -> 86.4 us
    pallas_call x1, Pallas kernels: 86.2 us -> 84.6 us  [shards(): pl.pallas_call(functools.partial(kernel, sizes), out_shape=(jax.ShapeDtyp...]
where the time goes in v5:
time: 87.2 us; the launch traced here: 87 us
  Pallas kernels  86.4 us (99%)
    pallas_call x1, Pallas kernels, shards(): pl.pallas_call(functools.partial(kernel, sizes), out_shape=(jax.ShapeDtyp...  84.6 us
    pallas_call x1, Pallas kernels, shards(): pl.pallas_call(relay, out_shape=(jax.ShapeDtypeStruct(tokens.shape, BF16)...  1.84 us

profile of v5, /device:TPU:1, one launch (start us, length us, event | category | flops | bytes accessed | tf_op | source)
XLA Modules:
  0.0 87.0 jit_solution(15917715494422600032)
XLA Ops:
  0.6 84.6 %hourglass.1 = (bf16[128,2048]{1,0:T(8,128)(2,1)}, f32[4,2048]{1,0:T(4,128)}) custom-call(bf16[128,2048]{1,0:T(8,128)(2,1)} %tok.1, bf16[128,2048]{1,0:T(8,128)(2,1)} %gout.1, f32[1,2048]{1,0:T(1,128)} %bitcast.4, f32[1,2048]{1,0:T(1,128)} %bitcast.5, f32[1,2048]{1,0:T(1,128)} %bitcast.6, f32[1,2048]{1,0:T(1,128)} %bitcast.7), custom_call_target="tpu_custom_call" | custom-call | tf_op jit(solution)/shard_map/hourglass/pallas_call | solution.py:615
  85.2 1.8 %relay.1 = (bf16[128,2048]{1,0:T(8,128)(2,1)}, f32[4,2048]{1,0:T(4,128)}) custom-call(bf16[128,2048]{1,0:T(8,128)(2,1)} %get-tuple-element.4.first, f32[4,2048]{1,0:T(4,128)} %get-tuple-element.5.second), custom_call_target="tpu_custom_call" | custom-call | tf_op jit(solution)/shard_map/relay/pallas_call | solution.py:634
